TPU v7x, 256 devices: a whole 4x4x8 slice. The times are simulated.
256 devices in a mesh: tgt: 8 (over y, x_lo), src: 32 (over z, x_hi, core).
Axes of the slice: x: 4 (x_hi: 2, x_lo: 2; x = x_hi * 2 + x_lo), y: 4, z: 8, core: 2. Of those that a mesh axis runs over, the one named last changes fastest.
Arguments:
- history: bfloat16 [16384, 2048], P(('src', 'tgt')), may hold values from -6 to 6
- kernel: bfloat16 [16, 32, 512, 4096], P('tgt', 'src'), may hold values from -0.03125 to 0.03125
- delays: int32 [16, 32], P('tgt', 'src'), may hold values from 0 to 120
- tile_mask: int32 [16, 32], P('tgt', 'src'), may hold values 0 or 1
Outputs:
- incoming: float32 [16, 512, 1024], P('tgt', 'src')
All inputs are finite; a program needn't handle non-finite values. No bound on the sum of `tile_mask` on one device may be relied on, other than what follows from the above.
Results may differ from a plain program's by a relative error of at most 0.0003.
Values may be sent and summed in bfloat16 or wider, within the bound.
No kernel may reach another device: no remote copies, remote signals or barrier semaphores. Data moves between devices by JAX's collectives and lax.ppermute only.
A program may use at most 64 MiB of HBM per device.

v0:
```python
import jax
import jax.numpy as jnp
from jax import lax
from jax.sharding import PartitionSpec as P

B = 512
TAPS = 8
H = 128
E = 16
S = 64


def compute_term(kernel_tile, source, tile_delay):
    padded = jnp.pad(source, ((0, 0), (0, S * E)))
    running = jnp.zeros((B, S * E), jnp.float32)
    for tap_index in range(TAPS):
        first_column = (H - tile_delay - tap_index) * E
        window = lax.dynamic_slice_in_dim(padded, first_column, S * E, 1)
        running = running + jnp.dot(
            kernel_tile[:, tap_index * B : (tap_index + 1) * B],
            window,
            preferred_element_type=jnp.float32,
        )
    return running


def body(history, kernel, delays, tile_mask):
    gathered = lax.all_gather(history, "tgt", axis=0, tiled=True)
    tgt_tiles = kernel.shape[0]

    def target_tile(index):
        operands = (kernel[index, 0], gathered, delays[index, 0])
        term = tile_mask[index, 0].astype(jnp.float32) * compute_term(*operands)
        return term

    partials = jnp.stack([target_tile(index) for index in range(tgt_tiles)])
    return lax.psum_scatter(partials, "src", scatter_dimension=1, tiled=True)


def solution(mesh):
    placed = (
        P(("src", "tgt"), None),
        P("tgt", "src", None, None),
        P("tgt", "src"),
        P("tgt", "src"),
    )
    return jax.shard_map(
        body, mesh=mesh, in_specs=placed, out_specs=P("tgt", "src", None), check_vma=False
    )
```

profile of v0, /device:TPU:1, one launch (start us, length us, event | category | flops | bytes accessed | tf_op | source)
XLA Modules:
  0.0 401.6 jit_solution(10008407857600112089)
XLA Ops:
  6.5 0.0 all-gather.2.cloned.1.call-start
  6.5 0.7 all-gather.2.cloned.1.call-update
  7.3 0.0 all-reduce.4.cloned.1.call-start
  7.3 1.4 fusion.63
  19.4 1.3 fusion.62
  22.1 6.0 %slice_bitcast_fusion.1 = (bf16[512,4096]{1,0:T(8,128)(2,1)}, bf16[512,4096]{1,0:T(8,128)(2,1)}) fusion(bf16[2,1,512,4096]{3,2,1,0:T(8,128)(2,1)} %param.5), kind=kLoop, calls=%fused_computation.18 | loop fusion | bytes 16777216 | tf_op jit(solution)/shard_map/squeeze | solution.py:32
  28.1 38.7 %all-gather.2.cloned.1.call-done = bf16[512,2048]{1,0:T(8,128)(2,1)} async-done(((bf16[64,2048]{1,0:T(8,128)(2,1)}), bf16[512,2048]{1,0:T(8,128)(2,1)}) %all-gather.2.cloned.1.call-update) | async-done | bytes 2097168 | tf_op jit(solution)/shard_map/all_gather | solution.py:28
  66.9 0.0 copy-start
  66.9 2.7 fusion
  69.5 0.0 copy-done
  69.5 0.0 copy-start.2
  69.6 2.6 fusion.1
  72.1 0.0 copy-done.2
  72.1 1.4 fusion.2
  73.5 1.4 fusion.3
  74.9 1.4 fusion.4
  76.3 1.4 fusion.5
  77.7 0.0 copy-start.1
  77.7 1.4 fusion.6
  79.1 0.8 copy-done.1
  79.9 1.4 fusion.10
  81.3 1.4 fusion.11
  82.7 1.4 fusion.12
  84.0 1.4 fusion.7
  85.4 1.6 fusion.8
  87.0 2.7 fusion.9
  89.7 2.7 fusion.13
  92.4 3.0 multiply_bitcast_fusion.1
  95.4 0.0 copy-start.3
  95.4 4.2 %multiply_bitcast_fusion = f32[1,512,1024]{1,2,0:T(8,128)S(1)} fusion(f32[1024,512]{1,0:T(8,128)} %fusion.13, f32[1024,512]{1,0:T(8,128)S(1)} %fusion.12, f32[1024,512]{1,0:T(8,128)S(1)} %fusion.11, f32[1024,512]{1,0:T(8,128)S(1)} %fusion.10, f32[1024,512]{1,0:T(8,128)} %fusion.9, f32[1024,512]{1,0:T(8,128)S(1)} %fusion.7, f32[1024,512]{1,0:T(8,128)S(1)} %fusion.8, ...), kind=kOutput, calls=%fused_computation.19 | convolution fusion | flops 541065216 | bytes 19398664 | tf_op jit(solution)/shard_map/dot_general | solution.py:19
  99.6 0.0 copy-done.3
  99.6 2.4 pad_maximum_fusion
  102.0 7.3 %copy.6 = f32[2,512,1024]{2,0,1:T(2,128)} copy(f32[2,512,1024]{1,2,0:T(8,128)} %pad_maximum_fusion) | data formatting | bytes 8388608 | tf_op jit(solution)/shard_map/stack | solution.py:36
  109.3 0.0 copy-start.4
  109.3 0.0 all-reduce.4.cloned.1.call-update
  109.4 0.6 copy-done.4
  110.0 0.6 dynamic-slice
  111.2 281.9 %all-reduce.4.cloned.1.call-done = f32[2,512,1024]{2,0,1:T(2,128)} async-done(((f32[2,512,1024]{2,0,1:T(2,128)}), f32[2,512,1024]{2,0,1:T(2,128)}) %all-reduce.4.cloned.1.call-update) | async-done | bytes 4194320
  393.2 0.9 constant_dynamic-slice_fusion
  394.1 0.7 copy.7
Async XLA Ops:
  6.5 60.3 %all-gather.2.cloned.1.call-start = ((), (), s32[]{:S(2)}) async-start(), calls=%async_computation | async-start | bytes 2359296 | tf_op jit(solution)/shard_map/all_gather | solution.py:28
  7.3 385.9 %all-reduce.4.cloned.1.call-start = ((), (), s32[]{:S(2)}) async-start(), calls=%async_computation.1 | async-start | bytes 8388608
  66.9 2.7 copy-start
  69.5 2.6 copy-start.2
  77.7 2.2 copy-start.1
  95.4 4.2 %copy-start.3 = (f32[1,512,1024]{1,2,0:T(8,128)S(1)}, f32[1,512,1024]{1,2,0:T(8,128)}, u32[]{:S(2)}) copy-start(f32[1,512,1024]{1,2,0:T(8,128)} %multiply_bitcast_fusion.1) | copy-start | bytes 6291460
  109.3 0.7 copy-start.4
Sparse Core Ops, SparseCore 0:
  9.1 57.6 all-gather.1
  109.5 283.6 all-reduce.3
where the time goes:
time: 402 us
  waiting for transfers between devices  321 us (80%)
  matrix products  31.8 us (8%)
  between operations  26.3 us (7%)
  local copies, waits for them, and re-layouts  19.7 us (5%)
    unnamed x3, waiting for transfers between devices  283 us
    all_gather x1, waiting for transfers between devices, body(): gathered = lax.all_gather(history, 'tgt', axis=0, tiled=True)  38.7 us
    dot_general x16, matrix products, compute_term(): jnp.dot(kernel_tile[:, tap_index * B:(tap_index + 1) * B], window, prefer...  31.8 us
  transfers between devices with their start and end apart: 2, of which 2 were waited for; matrix products, arithmetic and copies ran while one was open for 2% of the time, Pallas kernels for 0%

commit v1 on v0

v1 whole, which is shorter than its diff:
```python
import jax
import jax.numpy as jnp
import numpy as np
from jax import lax
from jax.experimental import pallas as pl
from jax.experimental.pallas import tpu as pltpu
from jax.sharding import Mesh, PartitionSpec as P

B = 512
TAPS = 8
H = 128
E = 16
S = 64
LANES = 128
COLS = S * E
WIDE = H * E
STEPS_PER_VREG = LANES // E

NY, NX, NZ, NH, NC = 4, 2, 8, 2, 2
AXES = ("y", "xl", "z", "xh", "c")
SHAPE = (NY, NX, NZ, NH, NC)
OFFSETS = (1, -1, 2, -2, 3, -3, 4)
GROUP = 16
BLOCK_ROWS = NH * 2 * GROUP
MESSAGE = BLOCK_ROWS * COLS // LANES


def route(move):
    index = np.arange(np.prod(SHAPE)).reshape(SHAPE)
    pairs = []
    for here in np.ndindex(*SHAPE):
        there = tuple(p % n for p, n in zip(move(*here), SHAPE))
        pairs.append((int(index[here]), int(index[there])))
    return pairs


def shift(x, dy=0, dx=0, dz=0, dh=0, dc=0):
    def move(y, xl, z, xh, c):
        return (y + dy, xl + dx, z + (dz if c == 0 else -dz), xh + dh, c + dc)

    return lax.ppermute(x, AXES, route(move))


def multiply_body(first, last, *refs):
    info, delays, live = refs[:3]
    low, high = refs[3:5]
    taps = refs[5 : 5 + TAPS]
    rest = refs[5 + TAPS :]
    if first:
        before, rest = None, rest
    else:
        before, rest = rest[0], rest[1:]
    if last:
        keep, send, shifted = rest
    else:
        after, shifted = rest
    tile = pl.program_id(0)

    @pl.when(tile == 0)
    def _():
        shifted[:, :, WIDE:] = jnp.zeros((STEPS_PER_VREG, LANES, COLS), jnp.bfloat16)
        for ref, place in ((low, info[1]), (high, 64 - info[1])):
            value = ref[...]
            at = pl.multiple_of(place, 64)
            for j in range(STEPS_PER_VREG):
                moved = value if j == 0 else jnp.concatenate([value[:, j * E :], jnp.zeros((64, j * E), jnp.bfloat16)], 1)
                shifted[j, pl.ds(at, 64), :WIDE] = moved

    delay = delays[tile]
    windows = []
    for tap in range(TAPS):
        step = H - delay - tap
        column = pl.multiple_of((step // STEPS_PER_VREG) * LANES, LANES)
        windows.append(shifted[step % STEPS_PER_VREG, :, pl.ds(column, COLS)])
    left = jnp.concatenate([tap[0, 0] for tap in taps], 1)
    total = jnp.dot(left, jnp.concatenate(windows, 0), preferred_element_type=jnp.float32)
    if before is not None:
        total = total + before[0]
    if not last:
        after[0] = total
        return
    total = total * live[tile].astype(jnp.float32)
    core = info[2]
    for z in range(NZ):
        for h in range(NH):
            row = ((z * NH + h) * NC) * GROUP
            one, two = total[row : row + GROUP], total[row + GROUP : row + 2 * GROUP]
            keep[z, h, 0] = jnp.where(core == 0, one, two)
            send[z, h, 0] = jnp.where(core == 0, two, one)


def multiply(info, delays, live, kernel, low, high, before, last):
    first = before is None

    def tap_spec(tap):
        return pl.BlockSpec((1, 1, B, LANES), lambda i, info, d, m: (i, 0, 0, tap * (B // LANES) + info[0]))

    half = pl.BlockSpec((64, WIDE), lambda i, *_: (0, 0))
    whole = pl.BlockSpec((1, B, COLS), lambda i, *_: (i, 0, 0))
    in_specs = [half, half] + [tap_spec(tap) for tap in range(TAPS)]
    operands = [low, high] + [kernel] * TAPS
    if not first:
        in_specs.append(whole)
        operands.append(before)
    if last:
        parts = pl.BlockSpec((NZ, NH, 1, GROUP, COLS), lambda i, *_: (0, 0, i, 0, 0))
        out_specs = [parts, parts]
        out_shape = [jax.ShapeDtypeStruct((NZ, NH, 2, GROUP, COLS), jnp.float32)] * 2
    else:
        out_specs = whole
        out_shape = jax.ShapeDtypeStruct((2, B, COLS), jnp.float32)
    return pl.pallas_call(
        lambda *refs: multiply_body(first, last, *refs),
        grid_spec=pltpu.PrefetchScalarGridSpec(
            num_scalar_prefetch=3,
            grid=(2,),
            in_specs=in_specs,
            out_specs=out_specs,
            scratch_shapes=[pltpu.VMEM((STEPS_PER_VREG, LANES, WIDE + COLS), jnp.bfloat16)],
        ),
        out_shape=out_shape,
        compiler_params=pltpu.CompilerParams(vmem_limit_bytes=40 << 20),
        name="multiply",
    )(info, delays, live, *operands)


def power_of_two(exponent):
    size = jnp.abs(exponent)
    result = jnp.ones(exponent.shape, jnp.float32)
    for bit in range(7):
        up, down = float(2.0 ** (1 << bit)), float(2.0 ** -(1 << bit))
        factor = jnp.where(exponent < 0, down, up)
        result = jnp.where((size >> bit) & 1 == 1, result * factor, result)
    return result


def encode_body(info, keep, get, own, *messages):
    z, sign = info[3], info[4]
    own[...] = keep[z] + get[z]
    for offset, message in zip(OFFSETS, messages):
        there = (z + sign * offset + NZ) % NZ
        scales = []
        for group in range(NH * 2):
            h, t = divmod(group, 2)
            value = keep[there, h, t] + get[there, h, t]
            peak = jnp.max(jnp.abs(value), axis=(0, 1), keepdims=True)
            peak = jnp.broadcast_to(peak, (1, LANES))
            exponent = jnp.ceil(jnp.log2(jnp.maximum(peak, 1e-30))).astype(jnp.int32) - 15
            scales.append(exponent)
            inverse = jnp.broadcast_to(power_of_two(-exponent), (GROUP, LANES))
            for j in range(COLS // LANES):
                scaled = jnp.clip(jnp.round(value[:, j * LANES : (j + 1) * LANES] * inverse), -32767.0, 32767.0)
                row = (group * (COLS // LANES) + j) * GROUP
                message[row : row + GROUP] = scaled.astype(jnp.int32).astype(jnp.int16)
        rows = lax.broadcasted_iota(jnp.int32, (GROUP, LANES), 0) // 4
        packed = jnp.zeros((GROUP, LANES), jnp.int32)
        for group, exponent in enumerate(scales):
            packed = jnp.where(rows == group, jnp.broadcast_to(exponent, (GROUP, LANES)), packed)
        message[MESSAGE:] = packed.astype(jnp.int16)


def encode(info, keep, get):
    return pl.pallas_call(
        encode_body,
        in_specs=[pl.BlockSpec(memory_space=pltpu.SMEM)] + [pl.BlockSpec(memory_space=pltpu.VMEM)] * 2,
        out_shape=[jax.ShapeDtypeStruct((NH, 2, GROUP, COLS), jnp.float32)]
        + [jax.ShapeDtypeStruct((MESSAGE + GROUP, LANES), jnp.int16)] * len(OFFSETS),
        compiler_params=pltpu.CompilerParams(vmem_limit_bytes=24 << 20),
        name="encode",
    )(info, keep, get)


def decode_body(info, own, *refs):
    messages, mine, other = refs[: len(OFFSETS)], refs[-2], refs[-1]
    units = []
    for message in messages:
        packed = message[MESSAGE:].astype(jnp.int32)
        units.append([power_of_two(packed[4 * group : 4 * group + 1]) for group in range(NH * 2)])
    for t in range(2):
        for j in range(COLS // LANES):
            sums = []
            for h in range(NH):
                group = h * 2 + t
                row = (group * (COLS // LANES) + j) * GROUP
                total = own[h, t, :, j * LANES : (j + 1) * LANES]
                for message, unit in zip(messages, units):
                    part = message[row : row + GROUP].astype(jnp.int32).astype(jnp.float32)
                    total = total + part * jnp.broadcast_to(unit[group], (GROUP, LANES))
                sums.append(total)
            here = info[5] == 0
            mine[t, :, j * LANES : (j + 1) * LANES] = jnp.where(here, sums[0], sums[1])
            other[t, :, j * LANES : (j + 1) * LANES] = jnp.where(here, sums[1], sums[0])


def decode(info, own, messages):
    return pl.pallas_call(
        decode_body,
        in_specs=[pl.BlockSpec(memory_space=pltpu.SMEM)] + [pl.BlockSpec(memory_space=pltpu.VMEM)] * (1 + len(OFFSETS)),
        out_shape=[jax.ShapeDtypeStruct((2, GROUP, COLS), jnp.float32)] * 2,
        compiler_params=pltpu.CompilerParams(vmem_limit_bytes=24 << 20),
        name="decode",
    )(info, own, *messages)


def body(history, kernel, delays, tile_mask):
    y, xl, z, xh, c = (lax.axis_index(name) for name in AXES)
    delays, live = delays[:, 0], tile_mask[:, 0]
    here = history
    two_far = shift(here, dy=2, dx=1)
    two = shift(here, dy=2)
    up_far = shift(here, dy=1, dx=1)
    up = shift(here, dy=1)
    down_far = shift(here, dy=-1, dx=1)
    down = shift(here, dy=-1)
    beside = shift(here, dx=1)

    def info(block):
        return jnp.stack([block % NY, xl * 64, c, z, 1 - 2 * c, xh]).astype(jnp.int32)

    total = None
    for block, low, high, last in (
        (y + 2, two, two_far, False),
        (y + 3, up, up_far, False),
        (y + 1, down, down_far, False),
        (y, here, beside, True),
    ):
        total = multiply(info(block), delays, live, kernel, low, high, total, last)
    keep, send = total
    get = shift(send, dc=1)
    own, *messages = encode(info(y), keep, get)
    received = [shift(message, dz=offset) for offset, message in zip(OFFSETS, messages)]
    mine, other = decode(info(y), own, received)
    return mine + shift(other, dh=1)


def solution(mesh):
    fine = Mesh(mesh.devices.reshape(SHAPE), AXES)
    tgt, src = ("y", "xl"), ("z", "xh", "c")
    placed = (
        P(src + tgt, None),
        P(tgt, src, None, None),
        P(tgt, src),
        P(tgt, src),
    )
    return jax.shard_map(body, mesh=fine, in_specs=placed, out_specs=P(tgt, src, None), check_vma=False)
```

time: 402 us -> 97.4 us (0.24)
  waiting for transfers between devices: 321 us -> 35.7 us
  matrix products: 31.8 us -> 0 us
  starting transfers between devices: 0.04 us -> 30.2 us
  between operations: 26.3 us -> 0.14 us
  Pallas kernels: 0 us -> 25 us
  local copies, waits for them, and re-layouts: 19.7 us -> 5.05 us
    unnamed x3 -> x0, waiting for transfers between devices: 283 us -> none
    all_gather x1 -> x0, waiting for transfers between devices: 38.7 us -> none  [body(): gathered = lax.all_gather(history, 'tgt', axis=0, tiled=True)]
    ppermute x0 -> x16, waiting for transfers between devices: none -> 35.7 us  [shift(): return lax.ppermute(x, AXES, route(move))]
    dot_general x16 -> x0, matrix products: 31.8 us -> none  [compute_term(): jnp.dot(kernel_tile[:, tap_index * B:(tap_index + 1) * B], window, prefer...]
    ppermute x0 -> x16, starting transfers between devices: none -> 30.2 us  [shift(): return lax.ppermute(x, AXES, route(move))]
    pallas_call x0 -> x6, Pallas kernels: none -> 25 us  [the longest x4 22.8 us: multiply(): pl.pallas_call(lambda *refs: multiply_body(first, last, *refs), grid_spec...]
    another operation x1 -> x4, local copies, waits for them, and re-layouts: 7.33 us -> 0.33 us  [info(): jnp.stack([block % NY, xl * 64, c, z, 1 - 2 * c, xh]).astype(jnp.int32)]
    squeeze x1 -> x0, local copies, waits for them, and re-layouts: 6.04 us -> none  [target_tile(): operands = (kernel[index, 0], gathered, delays[index, 0])]
  transfers between devices with their start and end apart: 2 -> 16, of which waited for: 2 -> 9; matrix products, arithmetic and copies ran while one was open for 2% -> 0% of each run, Pallas kernels for 0% -> 17%
where the time goes in v1:
time: 97.4 us; the launch traced here: 96.7 us
  waiting for transfers between devices  35.7 us (37%)
  starting transfers between devices  30.2 us (31%)
  Pallas kernels  25 us (26%)
  local copies, waits for them, and re-layouts  5.05 us (5%)
    ppermute x16, waiting for transfers between devices, shift(): return lax.ppermute(x, AXES, route(move))  35.7 us
    ppermute x16, starting transfers between devices, shift(): return lax.ppermute(x, AXES, route(move))  30.2 us
    pallas_call x4, Pallas kernels, multiply(): pl.pallas_call(lambda *refs: multiply_body(first, last, *refs), grid_spec...  22.8 us
    unnamed x12, local copies, waits for them, and re-layouts  4.72 us
  transfers between devices with their start and end apart: 16, of which 9 were waited for; matrix products, arithmetic and copies ran while one was open for 0% of the time, Pallas kernels for 17%

profile of v1, /device:TPU:1, one launch (start us, length us, event | category | flops | bytes accessed | tf_op | source)
XLA Modules:
  0.0 96.7 jit_solution(17547742966127438919)
XLA Ops:
  0.0 3.7 %collective-permute-start.5 = (bf16[64,2048]{1,0:T(8,128)(2,1)}, bf16[64,2048]{1,0:T(8,128)(2,1)S(1)}, u32[]{:S(2)}, u32[]{:S(2)}) collective-permute-start(bf16[64,2048]{1,0:T(8,128)(2,1)} %refs_3_.1), channel_id=1, source_target_pairs={{0,128},{1,129},{2,130},{3,131},{4,132},{5,133},{6,134},{7,135},{8... | collective-permute-start | bytes 786440 | tf_op jit(solution)/shard_map/ppermute | solution.py:41
  3.7 1.0 %collective-permute-start.6 = (bf16[64,2048]{1,0:T(8,128)(2,1)}, bf16[64,2048]{1,0:T(8,128)(2,1)S(1)}, u32[]{:S(2)}, u32[]{:S(2)}) collective-permute-start(bf16[64,2048]{1,0:T(8,128)(2,1)} %refs_3_.1), channel_id=1, source_target_pairs={{0,160},{1,161},{2,162},{3,163},{4,164},{5,165},{6,166},{7,167},{8... | collective-permute-start | bytes 786440 | tf_op jit(solution)/shard_map/ppermute | solution.py:41
  4.7 1.3 %collective-permute-start.3 = (bf16[64,2048]{1,0:T(8,128)(2,1)}, bf16[64,2048]{1,0:T(8,128)(2,1)S(1)}, u32[]{:S(2)}, u32[]{:S(2)}) collective-permute-start(bf16[64,2048]{1,0:T(8,128)(2,1)} %refs_3_.1), channel_id=1, source_target_pairs={{0,64},{1,65},{2,66},{3,67},{4,68},{5,69},{6,70},{7,71},{8,72},{9,... | collective-permute-start | bytes 786440 | tf_op jit(solution)/shard_map/ppermute | solution.py:41
  6.0 1.3 %collective-permute-start.4 = (bf16[64,2048]{1,0:T(8,128)(2,1)}, bf16[64,2048]{1,0:T(8,128)(2,1)S(1)}, u32[]{:S(2)}, u32[]{:S(2)}) collective-permute-start(bf16[64,2048]{1,0:T(8,128)(2,1)} %refs_3_.1), channel_id=1, source_target_pairs={{0,96},{1,97},{2,98},{3,99},{4,100},{5,101},{6,102},{7,103},{8,104... | collective-permute-start | bytes 786440 | tf_op jit(solution)/shard_map/ppermute | solution.py:41
  7.3 1.4 %collective-permute-start.1 = (bf16[64,2048]{1,0:T(8,128)(2,1)}, bf16[64,2048]{1,0:T(8,128)(2,1)S(1)}, u32[]{:S(2)}, u32[]{:S(2)}) collective-permute-start(bf16[64,2048]{1,0:T(8,128)(2,1)} %refs_3_.1), channel_id=1, source_target_pairs={{0,192},{1,193},{2,194},{3,195},{4,196},{5,197},{6,198},{7,199},{8... | collective-permute-start | bytes 786440 | tf_op jit(solution)/shard_map/ppermute | solution.py:41
  8.7 12.1 %collective-permute-done.5.refs_3_ = bf16[64,2048]{1,0:T(8,128)(2,1)S(1)} collective-permute-done((bf16[64,2048]{1,0:T(8,128)(2,1)}, bf16[64,2048]{1,0:T(8,128)(2,1)S(1)}, u32[]{:S(2)}, u32[]{:S(2)}) %collective-permute-start.5) | collective-permute-done | bytes 262176 | tf_op jit(solution)/shard_map/ppermute | solution.py:41
  20.8 0.0 collective-permute-start.2
  20.8 0.0 collective-permute-done.6.refs_4_
  20.8 1.5 %collective-permute-start = (bf16[64,2048]{1,0:T(8,128)(2,1)}, bf16[64,2048]{1,0:T(8,128)(2,1)S(1)}, u32[]{:S(2)}, u32[]{:S(2)}) collective-permute-start(bf16[64,2048]{1,0:T(8,128)(2,1)} %refs_3_.1), channel_id=1, source_target_pairs={{0,32},{1,33},{2,34},{3,35},{4,36},{5,37},{6,38},{7,39},{8,40},{9,... | collective-permute-start | bytes 786440 | tf_op jit(solution)/shard_map/ppermute | solution.py:41
  22.2 0.1 stack.38.refs_0_
  22.3 0.1 stack.36.refs_0_
  22.4 0.1 stack.34.refs_0_
  22.5 0.1 stack.32.refs_0_.info
  22.6 0.0 copy-start
  22.6 3.4 %copy-done = bf16[2,1,512,4096]{3,2,1,0:T(8,128)(2,1)S(1)} copy-done((bf16[2,1,512,4096]{3,2,1,0:T(8,128)(2,1)S(1)}, bf16[2,1,512,4096]{3,2,1,0:T(8,128)(2,1)}, u32[]{:S(2)}) %copy-start) | copy-done | bytes 8388632
  25.9 0.0 copy-start.2
  26.0 0.7 copy-done.2
  26.6 0.0 copy-start.4
  26.6 0.7 copy-done.4
  27.3 0.0 copy-start.3
  27.3 5.0 %multiply.4.refs_13_ = f32[2,512,1024]{2,1,0:T(8,128)S(1)} custom-call(s32[6]{0:T(128)S(1)} %stack.38.refs_0_, s32[2]{0:T(128)S(1)} %bitcast.11, s32[2]{0:T(128)S(1)} %bitcast.15, bf16[64,2048]{1,0:T(8,128)(2,1)S(1)} %collective-permute-done.5.refs_3_, bf16[64,2048]{1,0:T(8,128)(2,1)S(1)} %collective-permute-done.6.refs_4_, ...), custom_call_target="tpu_custom_call" | custom-call | tf_op jit(solution)/shard_map/multiply/pallas_call | solution.py:112
  32.3 0.0 copy-start.5
  32.3 0.0 collective-permute-done.3.refs_3_
  32.3 0.0 collective-permute-done.4.refs_4_
  32.3 0.0 copy-done.3
  32.3 5.8 %multiply.5.refs_13_ = f32[2,512,1024]{2,1,0:T(8,128)S(1)} custom-call(s32[6]{0:T(128)S(1)} %stack.36.refs_0_, s32[2]{0:T(128)S(1)} %bitcast.12, s32[2]{0:T(128)S(1)} %bitcast.16, bf16[64,2048]{1,0:T(8,128)(2,1)S(1)} %collective-permute-done.3.refs_3_, bf16[64,2048]{1,0:T(8,128)(2,1)S(1)} %collective-permute-done.4.refs_4_, ...), custom_call_target="tpu_custom_call" | custom-call | tf_op jit(solution)/shard_map/multiply/pallas_call | solution.py:112
  38.2 0.0 copy-start.1
  38.2 0.0 collective-permute-done.1.refs_3_
  38.2 0.0 collective-permute-done.2.refs_4_
  38.2 0.0 copy-done.5
  38.2 5.8 %multiply.6.refs_13_ = f32[2,512,1024]{2,1,0:T(8,128)S(1)} custom-call(s32[6]{0:T(128)S(1)} %stack.34.refs_0_, s32[2]{0:T(128)S(1)} %bitcast.13, s32[2]{0:T(128)S(1)} %bitcast.17, bf16[64,2048]{1,0:T(8,128)(2,1)S(1)} %collective-permute-done.1.refs_3_, bf16[64,2048]{1,0:T(8,128)(2,1)S(1)} %collective-permute-done.2.refs_4_, ...), custom_call_target="tpu_custom_call" | custom-call | tf_op jit(solution)/shard_map/multiply/pallas_call | solution.py:112
  44.0 0.0 collective-permute-done.refs_4_
  44.0 0.0 copy-done.1
  44.0 6.1 %multiply.7 = (f32[8,2,2,16,1024]{4,3,2,1,0:T(8,128)S(1)}, f32[8,2,2,16,1024]{4,3,2,1,0:T(8,128)S(1)}) custom-call(s32[6]{0:T(128)S(1)} %stack.32.refs_0_.info, s32[2]{0:T(128)S(1)} %bitcast.14, s32[2]{0:T(128)S(1)} %bitcast.18, bf16[64,2048]{1,0:T(8,128)(2,1)S(1)} %copy-done.1, bf16[64,2048]{1,0:T(8,128)(2,1)S(1)} %collective-permute-done.refs_4_, ...), custom_call_target="tpu_custom_call" | custom-call | tf_op jit(solution)/shard_map/multiply/pallas_call | solution.py:112
  50.2 3.0 %collective-permute-start.7 = (f32[8,2,2,16,1024]{4,3,2,1,0:T(8,128)S(1)}, f32[8,2,2,16,1024]{4,3,2,1,0:T(8,128)S(1)}, u32[]{:S(2)}, u32[]{:S(2)}) collective-permute-start(f32[8,2,2,16,1024]{4,3,2,1,0:T(8,128)S(1)} %get-tuple-element.18), channel_id=1, source_target_pairs={{0,1},{1,0},{2,3},{3,2},{4,5},{5,4},{6,7},{7,6},{8,9},{9,8},{10,11... | collective-permute-start | bytes 6291464 | tf_op jit(solution)/shard_map/ppermute | solution.py:41
  53.2 3.8 %collective-permute-done.7.get = f32[8,2,2,16,1024]{4,3,2,1,0:T(8,128)S(1)} collective-permute-done((f32[8,2,2,16,1024]{4,3,2,1,0:T(8,128)S(1)}, f32[8,2,2,16,1024]{4,3,2,1,0:T(8,128)S(1)}, u32[]{:S(2)}, u32[]{:S(2)}) %collective-permute-start.7) | collective-permute-done | bytes 2097184 | tf_op jit(solution)/shard_map/ppermute | solution.py:41
  57.0 1.3 %encode.1 = (f32[2,2,16,1024]{3,2,1,0:T(8,128)S(1)}, s16[528,128]{1,0:T(8,128)(2,1)S(1)}, s16[528,128]{1,0:T(8,128)(2,1)S(1)}, s16[528,128]{1,0:T(8,128)(2,1)S(1...) custom-call(s32[6]{0:T(128)S(1)} %stack.32.refs_0_.info, ...), custom_call_target="tpu_custom_call" | custom-call | tf_op jit(solution)/shard_map/encode/pallas_call | solution.py:163
  58.3 6.1 %collective-permute-start.10 = (s16[528,128]{1,0:T(8,128)(2,1)S(1)}, s16[528,128]{1,0:T(8,128)(2,1)S(1)}, u32[]{:S(2)}, u32[]{:S(2)}) collective-permute-start(s16[528,128]{1,0:T(8,128)(2,1)S(1)} %get-tuple-element.22), channel_id=1, source_target_pairs={{0,8},{1,25},{2,10},{3,27},{4,12},{5,29},{6,14},{7,31},{8,16},{9,1... | collective-permute-start | bytes 405512 | tf_op jit(solution)/shard_map/ppermute | solution.py:41
  64.4 0.0 collective-permute-start.11
  64.4 2.8 %collective-permute-start.12 = (s16[528,128]{1,0:T(8,128)(2,1)S(1)}, s16[528,128]{1,0:T(8,128)(2,1)S(1)}, u32[]{:S(2)}, u32[]{:S(2)}) collective-permute-start(s16[528,128]{1,0:T(8,128)(2,1)S(1)} %get-tuple-element.24), channel_id=1, source_target_pairs={{0,12},{1,21},{2,14},{3,23},{4,16},{5,25},{6,18},{7,27},{8,20},{9,... | collective-permute-start | bytes 405512 | tf_op jit(solution)/shard_map/ppermute | solution.py:41
  67.2 0.5 collective-permute-start.13
  67.7 3.3 %collective-permute-start.14 = (s16[528,128]{1,0:T(8,128)(2,1)S(1)}, s16[528,128]{1,0:T(8,128)(2,1)S(1)}, u32[]{:S(2)}, u32[]{:S(2)}) collective-permute-start(s16[528,128]{1,0:T(8,128)(2,1)S(1)} %get-tuple-element.26), channel_id=1, source_target_pairs={{0,16},{1,17},{2,18},{3,19},{4,20},{5,21},{6,22},{7,23},{8,24},{9,... | collective-permute-start | bytes 405512 | tf_op jit(solution)/shard_map/ppermute | solution.py:41
  71.0 0.0 collective-permute-done.10.refs_2_
  71.0 2.2 %collective-permute-start.8 = (s16[528,128]{1,0:T(8,128)(2,1)S(1)}, s16[528,128]{1,0:T(8,128)(2,1)S(1)}, u32[]{:S(2)}, u32[]{:S(2)}) collective-permute-start(s16[528,128]{1,0:T(8,128)(2,1)S(1)} %get-tuple-element.20), channel_id=1, source_target_pairs={{0,4},{1,29},{2,6},{3,31},{4,8},{5,1},{6,10},{7,3},{8,12},{9,5},{1... | collective-permute-start | bytes 405512 | tf_op jit(solution)/shard_map/ppermute | solution.py:41
  73.2 1.3 %collective-permute-done.11.refs_3_ = s16[528,128]{1,0:T(8,128)(2,1)S(1)} collective-permute-done((s16[528,128]{1,0:T(8,128)(2,1)S(1)}, s16[528,128]{1,0:T(8,128)(2,1)S(1)}, u32[]{:S(2)}, u32[]{:S(2)}) %collective-permute-start.11) | collective-permute-done | bytes 135200 | tf_op jit(solution)/shard_map/ppermute | solution.py:41
  74.5 0.0 collective-permute-start.9
  74.5 9.5 %collective-permute-done.12.refs_4_ = s16[528,128]{1,0:T(8,128)(2,1)S(1)} collective-permute-done((s16[528,128]{1,0:T(8,128)(2,1)S(1)}, s16[528,128]{1,0:T(8,128)(2,1)S(1)}, u32[]{:S(2)}, u32[]{:S(2)}) %collective-permute-start.12) | collective-permute-done | bytes 135200 | tf_op jit(solution)/shard_map/ppermute | solution.py:41
  84.0 1.4 %collective-permute-done.13.refs_5_ = s16[528,128]{1,0:T(8,128)(2,1)S(1)} collective-permute-done((s16[528,128]{1,0:T(8,128)(2,1)S(1)}, s16[528,128]{1,0:T(8,128)(2,1)S(1)}, u32[]{:S(2)}, u32[]{:S(2)}) %collective-permute-start.13) | collective-permute-done | bytes 135200 | tf_op jit(solution)/shard_map/ppermute | solution.py:41
  85.4 0.4 collective-permute-done.14.refs_6_
  85.8 1.8 %collective-permute-done.8.refs_0_ = s16[528,128]{1,0:T(8,128)(2,1)S(1)} collective-permute-done((s16[528,128]{1,0:T(8,128)(2,1)S(1)}, s16[528,128]{1,0:T(8,128)(2,1)S(1)}, u32[]{:S(2)}, u32[]{:S(2)}) %collective-permute-start.8) | collective-permute-done | bytes 135200 | tf_op jit(solution)/shard_map/ppermute | solution.py:41
  87.6 1.6 %collective-permute-done.9.refs_1_ = s16[528,128]{1,0:T(8,128)(2,1)S(1)} collective-permute-done((s16[528,128]{1,0:T(8,128)(2,1)S(1)}, s16[528,128]{1,0:T(8,128)(2,1)S(1)}, u32[]{:S(2)}, u32[]{:S(2)}) %collective-permute-start.9) | collective-permute-done | bytes 135200 | tf_op jit(solution)/shard_map/ppermute | solution.py:41
  89.2 0.9 decode.1
  90.1 2.1 %collective-permute-start.15 = (f32[2,16,1024]{2,1,0:T(8,128)S(1)}, f32[2,16,1024]{2,1,0:T(8,128)S(1)}, u32[]{:S(2)}, u32[]{:S(2)}) collective-permute-start(f32[2,16,1024]{2,1,0:T(8,128)S(1)} %get-tuple-element.28), channel_id=1, source_target_pairs={{0,2},{1,3},{2,0},{3,1},{4,6},{5,7},{6,4},{7,5},{8,10},{9,11},{10,... | collective-permute-start | bytes 393224 | tf_op jit(solution)/shard_map/ppermute | solution.py:41
  92.2 3.8 %collective-permute-done.15 = f32[2,16,1024]{2,1,0:T(8,128)S(1)} collective-permute-done((f32[2,16,1024]{2,1,0:T(8,128)S(1)}, f32[2,16,1024]{2,1,0:T(8,128)S(1)}, u32[]{:S(2)}, u32[]{:S(2)}) %collective-permute-start.15) | collective-permute-done | bytes 131104 | tf_op jit(solution)/shard_map/ppermute | solution.py:41
  96.0 0.7 add.34
Async XLA Ops:
  0.0 20.8 %collective-permute-start.5 = (bf16[64,2048]{1,0:T(8,128)(2,1)}, bf16[64,2048]{1,0:T(8,128)(2,1)S(1)}, u32[]{:S(2)}, u32[]{:S(2)}) collective-permute-start(bf16[64,2048]{1,0:T(8,128)(2,1)} %refs_3_.1), channel_id=1, source_target_pairs={{0,128},{1,129},{2,130},{3,131},{4,132},{5,133},{6,134},{7,135},{8... | collective-permute-start | bytes 786440 | tf_op jit(solution)/shard_map/ppermute | solution.py:41
  3.7 17.0 %collective-permute-start.6 = (bf16[64,2048]{1,0:T(8,128)(2,1)}, bf16[64,2048]{1,0:T(8,128)(2,1)S(1)}, u32[]{:S(2)}, u32[]{:S(2)}) collective-permute-start(bf16[64,2048]{1,0:T(8,128)(2,1)} %refs_3_.1), channel_id=1, source_target_pairs={{0,160},{1,161},{2,162},{3,163},{4,164},{5,165},{6,166},{7,167},{8... | collective-permute-start | bytes 786440 | tf_op jit(solution)/shard_map/ppermute | solution.py:41
  4.7 27.6 %collective-permute-start.3 = (bf16[64,2048]{1,0:T(8,128)(2,1)}, bf16[64,2048]{1,0:T(8,128)(2,1)S(1)}, u32[]{:S(2)}, u32[]{:S(2)}) collective-permute-start(bf16[64,2048]{1,0:T(8,128)(2,1)} %refs_3_.1), channel_id=1, source_target_pairs={{0,64},{1,65},{2,66},{3,67},{4,68},{5,69},{6,70},{7,71},{8,72},{9,... | collective-permute-start | bytes 786440 | tf_op jit(solution)/shard_map/ppermute | solution.py:41
  6.0 26.3 %collective-permute-start.4 = (bf16[64,2048]{1,0:T(8,128)(2,1)}, bf16[64,2048]{1,0:T(8,128)(2,1)S(1)}, u32[]{:S(2)}, u32[]{:S(2)}) collective-permute-start(bf16[64,2048]{1,0:T(8,128)(2,1)} %refs_3_.1), channel_id=1, source_target_pairs={{0,96},{1,97},{2,98},{3,99},{4,100},{5,101},{6,102},{7,103},{8,104... | collective-permute-start | bytes 786440 | tf_op jit(solution)/shard_map/ppermute | solution.py:41
  7.3 30.9 %collective-permute-start.1 = (bf16[64,2048]{1,0:T(8,128)(2,1)}, bf16[64,2048]{1,0:T(8,128)(2,1)S(1)}, u32[]{:S(2)}, u32[]{:S(2)}) collective-permute-start(bf16[64,2048]{1,0:T(8,128)(2,1)} %refs_3_.1), channel_id=1, source_target_pairs={{0,192},{1,193},{2,194},{3,195},{4,196},{5,197},{6,198},{7,199},{8... | collective-permute-start | bytes 786440 | tf_op jit(solution)/shard_map/ppermute | solution.py:41
  20.8 17.4 %collective-permute-start.2 = (bf16[64,2048]{1,0:T(8,128)(2,1)}, bf16[64,2048]{1,0:T(8,128)(2,1)S(1)}, u32[]{:S(2)}, u32[]{:S(2)}) collective-permute-start(bf16[64,2048]{1,0:T(8,128)(2,1)} %refs_3_.1), channel_id=1, source_target_pairs={{0,224},{1,225},{2,226},{3,227},{4,228},{5,229},{6,230},{7,231},{8... | collective-permute-start | bytes 786440 | tf_op jit(solution)/shard_map/ppermute | solution.py:41
  20.8 23.3 %collective-permute-start = (bf16[64,2048]{1,0:T(8,128)(2,1)}, bf16[64,2048]{1,0:T(8,128)(2,1)S(1)}, u32[]{:S(2)}, u32[]{:S(2)}) collective-permute-start(bf16[64,2048]{1,0:T(8,128)(2,1)} %refs_3_.1), channel_id=1, source_target_pairs={{0,32},{1,33},{2,34},{3,35},{4,36},{5,37},{6,38},{7,39},{8,40},{9,... | collective-permute-start | bytes 786440 | tf_op jit(solution)/shard_map/ppermute | solution.py:41
  22.6 3.4 %copy-start = (bf16[2,1,512,4096]{3,2,1,0:T(8,128)(2,1)S(1)}, bf16[2,1,512,4096]{3,2,1,0:T(8,128)(2,1)}, u32[]{:S(2)}) copy-start(bf16[2,1,512,4096]{3,2,1,0:T(8,128)(2,1)} %refs_12_.7) | copy-start | bytes 25165828
  25.9 0.7 copy-start.2
  26.6 0.7 copy-start.4
  27.3 5.1 %copy-start.3 = (s32[2,1]{0,1:T(1,128)S(1)}, s32[2,1]{0,1:T(1,128)}, u32[]{:S(2)}) copy-start(s32[2,1]{0,1:T(1,128)} %param.6) | copy-start | bytes 28
  32.3 5.9 %copy-start.5 = (s32[2,1]{0,1:T(1,128)S(1)}, s32[2,1]{0,1:T(1,128)}, u32[]{:S(2)}) copy-start(s32[2,1]{0,1:T(1,128)} %param.7) | copy-start | bytes 28
  38.2 5.9 %copy-start.1 = (bf16[64,2048]{1,0:T(8,128)(2,1)S(1)}, bf16[64,2048]{1,0:T(8,128)(2,1)}, u32[]{:S(2)}) copy-start(bf16[64,2048]{1,0:T(8,128)(2,1)} %refs_3_.1) | copy-start | bytes 786436
  50.2 6.8 %collective-permute-start.7 = (f32[8,2,2,16,1024]{4,3,2,1,0:T(8,128)S(1)}, f32[8,2,2,16,1024]{4,3,2,1,0:T(8,128)S(1)}, u32[]{:S(2)}, u32[]{:S(2)}) collective-permute-start(f32[8,2,2,16,1024]{4,3,2,1,0:T(8,128)S(1)} %get-tuple-element.18), channel_id=1, source_target_pairs={{0,1},{1,0},{2,3},{3,2},{4,5},{5,4},{6,7},{7,6},{8,9},{9,8},{10,11... | collective-permute-start | bytes 6291464 | tf_op jit(solution)/shard_map/ppermute | solution.py:41
  58.3 12.7 %collective-permute-start.10 = (s16[528,128]{1,0:T(8,128)(2,1)S(1)}, s16[528,128]{1,0:T(8,128)(2,1)S(1)}, u32[]{:S(2)}, u32[]{:S(2)}) collective-permute-start(s16[528,128]{1,0:T(8,128)(2,1)S(1)} %get-tuple-element.22), channel_id=1, source_target_pairs={{0,8},{1,25},{2,10},{3,27},{4,12},{5,29},{6,14},{7,31},{8,16},{9,1... | collective-permute-start | bytes 405512 | tf_op jit(solution)/shard_map/ppermute | solution.py:41
  64.4 10.1 %collective-permute-start.11 = (s16[528,128]{1,0:T(8,128)(2,1)S(1)}, s16[528,128]{1,0:T(8,128)(2,1)S(1)}, u32[]{:S(2)}, u32[]{:S(2)}) collective-permute-start(s16[528,128]{1,0:T(8,128)(2,1)S(1)} %get-tuple-element.23), channel_id=1, source_target_pairs={{0,24},{1,9},{2,26},{3,11},{4,28},{5,13},{6,30},{7,15},{8,0},{9,17... | collective-permute-start | bytes 405512 | tf_op jit(solution)/shard_map/ppermute | solution.py:41
  64.4 19.5 %collective-permute-start.12 = (s16[528,128]{1,0:T(8,128)(2,1)S(1)}, s16[528,128]{1,0:T(8,128)(2,1)S(1)}, u32[]{:S(2)}, u32[]{:S(2)}) collective-permute-start(s16[528,128]{1,0:T(8,128)(2,1)S(1)} %get-tuple-element.24), channel_id=1, source_target_pairs={{0,12},{1,21},{2,14},{3,23},{4,16},{5,25},{6,18},{7,27},{8,20},{9,... | collective-permute-start | bytes 405512 | tf_op jit(solution)/shard_map/ppermute | solution.py:41
  67.2 18.2 %collective-permute-start.13 = (s16[528,128]{1,0:T(8,128)(2,1)S(1)}, s16[528,128]{1,0:T(8,128)(2,1)S(1)}, u32[]{:S(2)}, u32[]{:S(2)}) collective-permute-start(s16[528,128]{1,0:T(8,128)(2,1)S(1)} %get-tuple-element.25), channel_id=1, source_target_pairs={{0,20},{1,13},{2,22},{3,15},{4,24},{5,17},{6,26},{7,19},{8,28},{9,... | collective-permute-start | bytes 405512 | tf_op jit(solution)/shard_map/ppermute | solution.py:41
  67.7 18.1 %collective-permute-start.14 = (s16[528,128]{1,0:T(8,128)(2,1)S(1)}, s16[528,128]{1,0:T(8,128)(2,1)S(1)}, u32[]{:S(2)}, u32[]{:S(2)}) collective-permute-start(s16[528,128]{1,0:T(8,128)(2,1)S(1)} %get-tuple-element.26), channel_id=1, source_target_pairs={{0,16},{1,17},{2,18},{3,19},{4,20},{5,21},{6,22},{7,23},{8,24},{9,... | collective-permute-start | bytes 405512 | tf_op jit(solution)/shard_map/ppermute | solution.py:41
  71.0 16.6 %collective-permute-start.8 = (s16[528,128]{1,0:T(8,128)(2,1)S(1)}, s16[528,128]{1,0:T(8,128)(2,1)S(1)}, u32[]{:S(2)}, u32[]{:S(2)}) collective-permute-start(s16[528,128]{1,0:T(8,128)(2,1)S(1)} %get-tuple-element.20), channel_id=1, source_target_pairs={{0,4},{1,29},{2,6},{3,31},{4,8},{5,1},{6,10},{7,3},{8,12},{9,5},{1... | collective-permute-start | bytes 405512 | tf_op jit(solution)/shard_map/ppermute | solution.py:41
  74.5 14.7 %collective-permute-start.9 = (s16[528,128]{1,0:T(8,128)(2,1)S(1)}, s16[528,128]{1,0:T(8,128)(2,1)S(1)}, u32[]{:S(2)}, u32[]{:S(2)}) collective-permute-start(s16[528,128]{1,0:T(8,128)(2,1)S(1)} %get-tuple-element.21), channel_id=1, source_target_pairs={{0,28},{1,5},{2,30},{3,7},{4,0},{5,9},{6,2},{7,11},{8,4},{9,13},{1... | collective-permute-start | bytes 405512 | tf_op jit(solution)/shard_map/ppermute | solution.py:41
  90.1 5.9 %collective-permute-start.15 = (f32[2,16,1024]{2,1,0:T(8,128)S(1)}, f32[2,16,1024]{2,1,0:T(8,128)S(1)}, u32[]{:S(2)}, u32[]{:S(2)}) collective-permute-start(f32[2,16,1024]{2,1,0:T(8,128)S(1)} %get-tuple-element.28), channel_id=1, source_target_pairs={{0,2},{1,3},{2,0},{3,1},{4,6},{5,7},{6,4},{7,5},{8,10},{9,11},{10,... | collective-permute-start | bytes 393224 | tf_op jit(solution)/shard_map/ppermute | solution.py:41

commit v2 on v0

v2 whole, which is shorter than its diff:
```python
import functools

import jax
import jax.numpy as jnp
import numpy as np
from jax import lax
from jax.experimental import pallas as pl
from jax.experimental.pallas import tpu as pltpu
from jax.sharding import Mesh, PartitionSpec as P

B = 512
TAPS = 8
H = 128
E = 16
S = 64
LANES = 128
COLS = S * E
WIDE = H * E
STEPS_PER_VREG = LANES // E

NY, NX, NZ, NH, NC = 4, 2, 8, 2, 2
AXES = ("y", "xl", "z", "xh", "c")
SHAPE = (NY, NX, NZ, NH, NC)
GROUP = 16
UNITS = 8
FIRST_LIMIT = 40
COLUMN_BLOCKS = COLS // LANES
UNIT_ROWS = GROUP * COLUMN_BLOCKS
SHIFTED = (STEPS_PER_VREG, LANES, WIDE + COLS)


def route(move):
    index = np.arange(np.prod(SHAPE)).reshape(SHAPE)
    pairs = []
    for here in np.ndindex(*SHAPE):
        there = tuple(p % n for p, n in zip(move(*here), SHAPE))
        pairs.append((int(index[here]), int(index[there])))
    return pairs


def shift(x, dy=0, dx=0, dz=0, dh=0, dc=0):
    def move(y, xl, z, xh, c):
        return (y + dy, xl + dx, z + (dz if c == 0 else -dz), xh + dh, c + dc)

    return lax.ppermute(x, AXES, route(move))


def build_tail(shifted):
    shifted[:, :, WIDE:] = jnp.zeros((STEPS_PER_VREG, LANES, COLS), jnp.bfloat16)


def build_rows(ref, place, shifted):
    value = ref[...]
    at = pl.multiple_of(place, 64)
    for j in range(STEPS_PER_VREG):
        moved = value if j == 0 else jnp.concatenate([value[:, j * E :], jnp.zeros((64, j * E), jnp.bfloat16)], 1)
        shifted[j, pl.ds(at, 64), :WIDE] = moved


def build_shifted(info, low, high, shifted):
    build_tail(shifted)
    build_rows(low, info[1], shifted)
    build_rows(high, 64 - info[1], shifted)


def product(info, tile, turns, staged, all_shifted):
    weights, windows = [], []
    for turn, shifted in zip(turns, all_shifted):
        block = lax.rem(info[0] + turn, NY)
        for tap in range(TAPS):
            column = pl.multiple_of(tap * B + block * LANES, LANES)
            weights.append(staged[tile, :, pl.ds(column, LANES)])
            step = H - info[6 + tile] - tap
            column = pl.multiple_of((step // STEPS_PER_VREG) * LANES, LANES)
            windows.append(shifted[step % STEPS_PER_VREG, :, pl.ds(column, COLS)])
    left, right = jnp.concatenate(weights, 1), jnp.concatenate(windows, 0)
    return jnp.dot(left, right, preferred_element_type=jnp.float32)


def split(info, tile, total, keep, send, sums):
    sums[...] = total * info[8 + tile].astype(jnp.float32)
    core, z, sign, xh = info[2], info[3], info[4], info[5]
    for target, core, sign in ((keep, core, sign), (send, 1 - core, -sign)):
        for unit in range(UNITS):
            offset = unit // 2 + 1 if unit < 6 else (4, 0)[unit - 6]
            there = lax.rem(z + sign * offset + NZ, NZ)
            owner = unit % 2 if unit < 6 else core
            for half, side in enumerate((xh, 1 - xh)):
                row = pl.multiple_of(((there * NH + side) * NC + owner) * GROUP, GROUP)
                target[half, unit] = sums[pl.ds(row, GROUP), :]


def first_body(info, low, high, kernel, sum0, sum1, staged, shifted, arrived):
    copies = [pltpu.make_async_copy(kernel.at[tile, 0], staged.at[tile], arrived.at[tile]) for tile in range(2)]
    for copy in copies:
        copy.start()
    build_shifted(info, low, high, shifted)
    for tile, after in enumerate((sum0, sum1)):
        copies[tile].wait()
        after[...] = product(info, tile, (0,), staged, (shifted,))


def middle_body(turn, info, low, high, staged, before, after, shifted):
    build_shifted(info, low, high, shifted)
    after[...] = before[...] + product(info, 0, (turn,), staged, (shifted,))


def last_body(turns, info, low0, high0, low1, high1, staged, before, keep, send, shifted0, shifted1, sums):
    build_shifted(info, low0, high0, shifted0)
    build_shifted(info, low1, high1, shifted1)
    total = before[...] + product(info, 0, turns, staged, (shifted0, shifted1))
    split(info, 0, total, keep, send, sums)


def rest_body(turns, info, staged, before, *refs):
    keep, send, sums = refs[-3:]
    split(info, 1, before[...] + product(info, 1, turns, staged, refs[: len(turns)]), keep, send, sums)


NEAR = pl.BlockSpec(memory_space=pltpu.VMEM)
SMALL = pl.BlockSpec(memory_space=pltpu.SMEM)
TOTAL = jax.ShapeDtypeStruct((B, COLS), jnp.float32)
PARTS = jax.ShapeDtypeStruct((NH, UNITS, GROUP, COLS), jnp.float32)
COPIES = jax.ShapeDtypeStruct(SHIFTED, jnp.bfloat16)


def call(run, outs, operands, scratch=(), specs=None, limit=16, blocks=0, aliases=None):
    return pl.pallas_call(
        run,
        in_specs=specs or [SMALL] + [NEAR] * (len(operands) - 1),
        out_specs=[NEAR] * len(outs),
        out_shape=outs,
        scratch_shapes=scratch,
        input_output_aliases=aliases or {},
        compiler_params=pltpu.CompilerParams(vmem_limit_bytes=limit << 20),
        cost_estimate=pl.CostEstimate(
            flops=2 * B * COLS * TAPS * LANES * blocks, transcendentals=0, bytes_accessed=(4 << 20) if blocks else (1 << 20)
        ),
    )(*operands)


def power_of_two(exponent):
    size = jnp.abs(exponent)
    result = jnp.ones(exponent.shape, jnp.float32)
    for bit in range(7):
        up, down = float(2.0 ** (1 << bit)), float(2.0 ** -(1 << bit))
        factor = jnp.where(exponent < 0, down, up)
        result = jnp.where((size >> bit) & 1 == 1, result * factor, result)
    return result


def put(message, groups):
    exponents = []
    for index, value in enumerate(groups):
        peak = jnp.max(jnp.abs(value), axis=(0, 1), keepdims=True)
        peak = jnp.broadcast_to(peak, (1, LANES))
        exponent = jnp.ceil(jnp.log2(jnp.maximum(peak, 1e-30))).astype(jnp.int32) - 15
        exponents.append(exponent)
        inverse = jnp.broadcast_to(power_of_two(-exponent), (GROUP, LANES))
        for j in range(COLUMN_BLOCKS):
            scaled = jnp.clip(jnp.round(value[:, j * LANES : (j + 1) * LANES] * inverse), -32767.0, 32767.0)
            row = index * UNIT_ROWS + j * GROUP
            message[row : row + GROUP] = scaled.astype(jnp.int32).astype(jnp.int16)
    rows = lax.broadcasted_iota(jnp.int32, (GROUP, LANES), 0) // 2
    packed = jnp.zeros((GROUP, LANES), jnp.int32)
    for index, exponent in enumerate(exponents):
        packed = jnp.where(rows == index, jnp.broadcast_to(exponent, (GROUP, LANES)), packed)
    message[len(groups) * UNIT_ROWS :] = packed.astype(jnp.int16)


def units_of(message, count):
    packed = message[count * UNIT_ROWS :].astype(jnp.int32)
    return [jnp.broadcast_to(power_of_two(packed[2 * index : 2 * index + 1]), (GROUP, LANES)) for index in range(count)]


def part(message, unit, index, j):
    row = index * UNIT_ROWS + j * GROUP
    return message[row : row + GROUP].astype(jnp.int32).astype(jnp.float32) * unit[index]


def sent(count):
    return jax.ShapeDtypeStruct((count * UNIT_ROWS + GROUP, LANES), jnp.int16)


def across_body(info, keep, get, own, message):
    own[...] = keep[0] + get[0]
    put(message, [keep[1, unit] + get[1, unit] for unit in range(UNITS)])


def both_body(info, keep, get, one, two, three, four, base):
    def value(half, unit):
        return keep[half, unit] + get[half, unit]

    for k, message in enumerate((one, two, three)):
        put(message, [value(half, 2 * k + owner) for owner in range(2) for half in range(NH)])
    put(four, [value(half, 6) for half in range(NH)])
    for half in range(NH):
        base[half] = value(half, 7)


def along_body(info, own, come, one, two, three, four, base):
    unit = units_of(come, UNITS)

    def value(u):
        parts = [own[u, :, j * LANES : (j + 1) * LANES] + part(come, unit, u, j) for j in range(COLUMN_BLOCKS)]
        return jnp.concatenate(parts, 1)

    for k, message in enumerate((one, two, three)):
        put(message, [value(2 * k + owner) for owner in range(2)])
    put(four, [value(6)])
    base[...] = value(7)


def gather_body(info, base, one, two, three, four, stay, cross):
    units = [units_of(message, 4) for message in (one, two, three)]
    last = units_of(four, 2)
    for half, target in enumerate((stay, cross)):
        for j in range(COLUMN_BLOCKS):
            lanes = slice(j * LANES, (j + 1) * LANES)
            here = base[half, :, lanes] + part(four, last, half, j)
            for owner in range(2):
                parts = [part(m, u, owner * 2 + half, j) for m, u in zip((one, two, three), units)]
                extra = jnp.where(info[2] == owner, here, jnp.zeros_like(here))
                target[owner, :, lanes] = parts[0] + parts[1] + parts[2] + extra


def finish_body(info, base, stay, got, one, two, three, four, mine, other):
    core = info[2]
    units = [units_of(message, 2) for message in (one, two, three)]
    last = units_of(four, 1)
    for j in range(COLUMN_BLOCKS):
        lanes = slice(j * LANES, (j + 1) * LANES)
        sums, done = [], []
        for owner in range(2):
            parts = [part(m, u, owner, j) for m, u in zip((one, two, three), units)]
            sums.append(parts[0] + parts[1] + parts[2])
            done.append(stay[owner, :, lanes] + got[owner, :, lanes])
        here = base[:, lanes] + part(four, last, 0, j)
        mine[0, :, lanes] = jnp.where(core == 0, sums[0], sums[1]) + here
        other[0, :, lanes] = jnp.where(core == 0, sums[1], sums[0])
        mine[1, :, lanes] = jnp.where(core == 0, done[0], done[1])
        other[1, :, lanes] = jnp.where(core == 0, done[1], done[0])


def compute(history, kernel, delays, tile_mask):
    y, xl, z, xh, c = (lax.axis_index(name) for name in AXES)
    delays, live = delays.reshape(2), tile_mask.reshape(2)
    here = history
    beside = shift(here, dx=1)
    up = shift(here, dy=1)
    down = shift(here, dy=-1)
    two = shift(here, dy=2)
    up_far = shift(beside, dy=1)
    down_far = shift(beside, dy=-1)
    two_far = shift(two, dx=1)

    info = jnp.stack([y, xl * 64, c, z, 1 - 2 * c, xh]).astype(jnp.int32)
    info = jnp.concatenate([info, delays, live])
    sum0, sum1, staged = call(
        first_body,
        [TOTAL, TOTAL, jax.ShapeDtypeStruct((2, B, TAPS * B), jnp.bfloat16)],
        [info, here, beside, kernel],
        [pltpu.VMEM(SHIFTED, jnp.bfloat16), pltpu.SemaphoreType.DMA((2,))],
        [SMALL, NEAR, NEAR, pl.BlockSpec(memory_space=pl.ANY)],
        FIRST_LIMIT,
        2,
    )
    run = functools.partial(middle_body, 2)
    operands = [info, two, two_far, staged, sum0]
    sum0, two_copies = call(run, [TOTAL, COPIES], operands, blocks=1, aliases={4: 0})
    sums = [pltpu.VMEM((B, COLS), jnp.float32)]
    run = functools.partial(last_body, (3, 1))
    operands = [info, up, up_far, down, down_far, staged, sum0]
    keep0, send0, up_copies, down_copies = call(run, [PARTS, PARTS, COPIES, COPIES], operands, sums, blocks=2)
    get0 = shift(send0, dc=1)
    run = functools.partial(rest_body, (2, 3, 1))
    operands = [info, staged, sum1, two_copies, up_copies, down_copies]
    keep1, send1 = call(run, [PARTS, PARTS], operands, sums, blocks=3)
    get1 = shift(send1, dc=1)
    rows = jax.ShapeDtypeStruct((UNITS, GROUP, COLS), jnp.float32)
    own0, go0 = call(across_body, [rows, sent(UNITS)], [info, keep0, get0])
    come0 = shift(go0, dh=1)
    pair = jax.ShapeDtypeStruct((2, GROUP, COLS), jnp.float32)
    single = jax.ShapeDtypeStruct((GROUP, COLS), jnp.float32)
    *messages, base1 = call(both_body, [sent(4)] * 3 + [sent(2), pair], [info, keep1, get1])
    came1 = [shift(message, dz=offset) for offset, message in zip((1, 2, 3, 4), messages)]
    *messages, base0 = call(along_body, [sent(2)] * 3 + [sent(1), single], [info, own0, come0])
    came0 = [shift(message, dz=offset) for offset, message in zip((1, 2, 3, 4), messages)]
    stay, cross = call(gather_body, [pair, pair], [info, base1, *came1])
    got = shift(cross, dh=1)
    mine, other = call(finish_body, [pair, pair], [info, base0, stay, got, *came0])
    return mine + shift(other, dc=1)


def solution(mesh):
    fine = Mesh(mesh.devices.reshape(SHAPE), AXES)
    tgt, src = ("y", "xl"), ("z", "xh", "c")
    placed = (
        P(src + tgt, None),
        P(tgt, src, None, None),
        P(tgt, src),
        P(tgt, src),
    )
    return jax.shard_map(compute, mesh=fine, in_specs=placed, out_specs=P(tgt, src, None), check_vma=False)
```

time: 402 us -> 86 us (0.21)
  waiting for transfers between devices: 321 us -> 14.6 us
  starting transfers between devices: 0.04 us -> 46.5 us
  matrix products: 31.8 us -> 0 us
  between operations: 26.3 us -> 0.14 us
  Pallas kernels: 0 us -> 22.3 us
  local copies, waits for them, and re-layouts: 19.7 us -> 1.7 us
    unnamed x3 -> x0, waiting for transfers between devices: 283 us -> none
    ppermute x0 -> x20, starting transfers between devices: none -> 46.5 us  [shift(): return lax.ppermute(x, AXES, route(move))]
    all_gather x1 -> x0, waiting for transfers between devices: 38.7 us -> none  [body(): gathered = lax.all_gather(history, 'tgt', axis=0, tiled=True)]
    dot_general x16 -> x0, matrix products: 31.8 us -> none  [compute_term(): jnp.dot(kernel_tile[:, tap_index * B:(tap_index + 1) * B], window, prefer...]
    pallas_call x0 -> x9, Pallas kernels: none -> 22.3 us  [call(): pl.pallas_call(run, in_specs=specs or [SMALL] + [NEAR] * (len(operands) -...]
    ppermute x0 -> x20, waiting for transfers between devices: none -> 14.6 us  [shift(): return lax.ppermute(x, AXES, route(move))]
    another operation x1 -> x0, local copies, waits for them, and re-layouts: 7.33 us -> none  [body(): partials = jnp.stack([target_tile(index) for index in range(tgt_tiles)])]
    squeeze x1 -> x0, local copies, waits for them, and re-layouts: 6.04 us -> none  [target_tile(): operands = (kernel[index, 0], gathered, delays[index, 0])]
  transfers between devices with their start and end apart: 2 -> 20, of which waited for: 2 -> 4; matrix products, arithmetic and copies ran while one was open for 2% -> 1% of each run, Pallas kernels for 0% -> 20%
where the time goes in v2:
time: 86 us; the launch traced here: 85.9 us
  starting transfers between devices  46.5 us (54%)
  Pallas kernels  22.3 us (26%)
  waiting for transfers between devices  14.6 us (17%)
  local copies, waits for them, and re-layouts  1.7 us (2%)
    ppermute x20, starting transfers between devices, shift(): return lax.ppermute(x, AXES, route(move))  46.5 us
    pallas_call x9, Pallas kernels, call(): pl.pallas_call(run, in_specs=specs or [SMALL] + [NEAR] * (len(operands) -...  22.3 us
    ppermute x20, waiting for transfers between devices, shift(): return lax.ppermute(x, AXES, route(move))  14.6 us
  transfers between devices with their start and end apart: 20, of which 4 were waited for; matrix products, arithmetic and copies ran while one was open for 1% of the time, Pallas kernels for 20%

profile of v2, /device:TPU:1, one launch (start us, length us, event | category | flops | bytes accessed | tf_op | source)
XLA Modules:
  0.0 85.9 jit_solution(12276991255860444701)
XLA Ops:
  0.0 3.7 %collective-permute-start.5 = (bf16[64,2048]{1,0:T(8,128)(2,1)}, bf16[64,2048]{1,0:T(8,128)(2,1)S(1)}, u32[]{:S(2)}, u32[]{:S(2)}) collective-permute-start(bf16[64,2048]{1,0:T(8,128)(2,1)} %low.1), channel_id=1, source_target_pairs={{0,128},{1,129},{2,130},{3,131},{4,132},{5,133},{6,134},{7,135},{8... | collective-permute-start | bytes 786440 | tf_op jit(solution)/shard_map/ppermute | solution.py:45
  3.7 1.2 %collective-permute-start.1 = (bf16[64,2048]{1,0:T(8,128)(2,1)}, bf16[64,2048]{1,0:T(8,128)(2,1)S(1)}, u32[]{:S(2)}, u32[]{:S(2)}) collective-permute-start(bf16[64,2048]{1,0:T(8,128)(2,1)} %low.1), channel_id=1, source_target_pairs={{0,32},{1,33},{2,34},{3,35},{4,36},{5,37},{6,38},{7,39},{8,40},{9,... | collective-permute-start | bytes 786440 | tf_op jit(solution)/shard_map/ppermute | solution.py:45
  4.9 4.1 %collective-permute-done.5.low = bf16[64,2048]{1,0:T(8,128)(2,1)S(1)} collective-permute-done((bf16[64,2048]{1,0:T(8,128)(2,1)}, bf16[64,2048]{1,0:T(8,128)(2,1)S(1)}, u32[]{:S(2)}, u32[]{:S(2)}) %collective-permute-start.5) | collective-permute-done | bytes 262176 | tf_op jit(solution)/shard_map/ppermute | solution.py:45
  9.0 1.9 %collective-permute-start.6 = (bf16[64,2048]{1,0:T(8,128)(2,1)S(1)}, bf16[64,2048]{1,0:T(8,128)(2,1)S(1)}, u32[]{:S(2)}, u32[]{:S(2)}) collective-permute-start(bf16[64,2048]{1,0:T(8,128)(2,1)S(1)} %collective-permute-done.5.low), channel_id=1, source_target_pairs={{0,32},{1,33},{2,34},{3,35},{4,36},{5,37},{6,38},{7,39},{8,40},{9,... | collective-permute-start | bytes 786440 | tf_op jit(solution)/shard_map/ppermute | solution.py:45
  10.9 2.7 %collective-permute-start.3 = (bf16[64,2048]{1,0:T(8,128)(2,1)}, bf16[64,2048]{1,0:T(8,128)(2,1)S(1)}, u32[]{:S(2)}, u32[]{:S(2)}) collective-permute-start(bf16[64,2048]{1,0:T(8,128)(2,1)} %low.1), channel_id=1, source_target_pairs={{0,192},{1,193},{2,194},{3,195},{4,196},{5,197},{6,198},{7,199},{8... | collective-permute-start | bytes 786440 | tf_op jit(solution)/shard_map/ppermute | solution.py:45
  13.7 0.0 collective-permute-start
  13.7 0.8 concatenate.3.info
  14.4 0.0 collective-permute-done.1.high
  14.4 2.8 %collective-permute-start.4 = (bf16[64,2048]{1,0:T(8,128)(2,1)S(1)}, bf16[64,2048]{1,0:T(8,128)(2,1)S(1)}, u32[]{:S(2)}, u32[]{:S(2)}) collective-permute-start(bf16[64,2048]{1,0:T(8,128)(2,1)S(1)} %collective-permute-done.1.high), channel_id=1, source_target_pairs={{0,192},{1,193},{2,194},{3,195},{4,196},{5,197},{6,198},{7,199},{8... | collective-permute-start | bytes 786440 | tf_op jit(solution)/shard_map/ppermute | solution.py:45
  17.2 0.0 collective-permute-start.2
  17.2 0.0 copy-start
  17.2 0.9 %copy-done = bf16[64,2048]{1,0:T(8,128)(2,1)S(1)} copy-done((bf16[64,2048]{1,0:T(8,128)(2,1)S(1)}, bf16[64,2048]{1,0:T(8,128)(2,1)}, u32[]{:S(2)}) %copy-start) | copy-done | bytes 262168
  18.1 6.1 %shard_map.46 = (f32[512,1024]{1,0:T(8,128)S(1)}, f32[512,1024]{1,0:T(8,128)S(1)}, bf16[2,512,4096]{2,1,0:T(8,128)(2,1)S(1)}) custom-call(s32[10]{0:T(128)S(1)} %concatenate.3.info, bf16[64,2048]{1,0:T(8,128)(2,1)S(1)} %copy-done, bf16[64,2048]{1,0:T(8,128)(2,1)S(1)} %collective-permute-done.1.high, bf16[2,1,512,4096]{3,2,1,0:T(8,128)(2,1)} %kernel.1), custom_call_target="tpu_custom_call" | custom-call | flops 2147483648 | bytes 4194304 | tf_op jit(solution)/shard_map/pallas_call | solution.py:128
  24.3 0.0 collective-permute-done.6.high
  24.3 3.1 %shard_map.47 = (f32[512,1024]{1,0:T(8,128)S(1)}, bf16[8,128,3072]{2,1,0:T(8,128)(2,1)S(1)}) custom-call(s32[10]{0:T(128)S(1)} %concatenate.3.info, bf16[64,2048]{1,0:T(8,128)(2,1)S(1)} %collective-permute-done.5.low, bf16[64,2048]{1,0:T(8,128)(2,1)S(1)} %collective-permute-done.6.high, ...), custom_call_target="tpu_custom_call", output_to_operand_aliasing={{0}: (4, {})} | custom-call | flops 1073741824 | bytes 4194304 | tf_op jit(solution)/shard_map/pallas_call | solution.py:128
  27.4 0.0 collective-permute-done.3.low1
  27.4 0.0 collective-permute-done.low0
  27.4 0.0 collective-permute-done.4.high1
  27.4 0.0 collective-permute-done.2.high0
  27.4 4.9 %shard_map.48 = (f32[2,8,16,1024]{3,2,1,0:T(8,128)S(1)}, f32[2,8,16,1024]{3,2,1,0:T(8,128)S(1)}, bf16[8,128,3072]{2,1,0:T(8,128)(2,1)S(1)}, bf16[8,128,3072]{2,1,0:T(8,128)(2,1)S(1)}) custom-call(s32[10]{0:T(128)S(1)} %concatenate.3.info, bf16[64,2048]{1,0:T(8,128)(2,1)S(1)} %collective-permute-done.low0, bf16[64,2048]{1,0:T(8,128)(2,1)S(1)} %collective-permute-done.2.high0, ...), custom_call_target="tpu_custom_call" | custom-call | flops 2147483648 | bytes 4194304 | tf_op jit(solution)/shard_map/pallas_call | solution.py:128
  32.3 2.7 %collective-permute-start.7 = (f32[2,8,16,1024]{3,2,1,0:T(8,128)S(1)}, f32[2,8,16,1024]{3,2,1,0:T(8,128)S(1)}, u32[]{:S(2)}, u32[]{:S(2)}) collective-permute-start(f32[2,8,16,1024]{3,2,1,0:T(8,128)S(1)} %get-tuple-element.36), channel_id=1, source_target_pairs={{0,1},{1,0},{2,3},{3,2},{4,5},{5,4},{6,7},{7,6},{8,9},{9,8},{10,11... | collective-permute-start | bytes 3145736 | tf_op jit(solution)/shard_map/ppermute | solution.py:45
  35.1 4.2 %shard_map.51 = (f32[2,8,16,1024]{3,2,1,0:T(8,128)S(1)}, f32[2,8,16,1024]{3,2,1,0:T(8,128)S(1)}) custom-call(s32[10]{0:T(128)S(1)} %concatenate.3.info, bf16[2,512,4096]{2,1,0:T(8,128)(2,1)S(1)} %get-tuple-element.32.staged, f32[512,1024]{1,0:T(8,128)S(1)} %get-tuple-element.40.before, bf16[8,128,3072]{2,1,0:T(8,128)(2,1)S(1)} %get-tuple-element.41.refs_0_, ...), custom_call_target="tpu_custom_call" | custom-call | flops 3221225472 | bytes 4194304 | tf_op jit(solution)/shard_map/pallas_call | solution.py:128
  39.2 0.3 collective-permute-start.9
  39.5 0.0 collective-permute-done.7.get
  39.6 0.9 %shard_map.49 = (f32[8,16,1024]{2,1,0:T(8,128)S(1)}, s16[1040,128]{1,0:T(8,128)(2,1)S(1)}) custom-call(s32[10]{0:T(128)S(1)} %concatenate.3.info, f32[2,8,16,1024]{3,2,1,0:T(8,128)S(1)} %get-tuple-element.35.keep, f32[2,8,16,1024]{3,2,1,0:T(8,128)S(1)} %collective-permute-done.7.get), custom_call_target="tpu_custom_call" | custom-call | bytes 1048576 | tf_op jit(solution)/shard_map/pallas_call | solution.py:128
  40.5 2.5 %collective-permute-start.8 = (s16[1040,128]{1,0:T(8,128)(2,1)S(1)}, s16[1040,128]{1,0:T(8,128)(2,1)S(1)}, u32[]{:S(2)}, u32[]{:S(2)}) collective-permute-start(s16[1040,128]{1,0:T(8,128)(2,1)S(1)} %get-tuple-element.38), channel_id=1, source_target_pairs={{0,2},{1,3},{2,0},{3,1},{4,6},{5,7},{6,4},{7,5},{8,10},{9,11},{10,... | collective-permute-start | bytes 798728 | tf_op jit(solution)/shard_map/ppermute | solution.py:45
  43.0 0.0 collective-permute-done.9.get
  43.0 1.0 %shard_map.52 = (s16[528,128]{1,0:T(8,128)(2,1)S(1)}, s16[528,128]{1,0:T(8,128)(2,1)S(1)}, s16[528,128]{1,0:T(8,128)(2,1)S(1)}, s16[272,128]{1,0:T(8,128)(2,1)S(1)}, f32[2,16,1024]{2,1,0:T(8,128)S(1)}) custom-call(s32[10]{0:T(128)S(1)} %concatenate.3.info, f32[2,8,16,1024]{3,2,1,0:T(8,128)S(1)} %get-tuple-element.44.keep, ...), custom_call_target="tpu_custom_call" | custom-call | bytes 1048576 | tf_op jit(solution)/shard_map/pallas_call | solution.py:128
  44.0 5.6 %collective-permute-start.10 = (s16[528,128]{1,0:T(8,128)(2,1)S(1)}, s16[528,128]{1,0:T(8,128)(2,1)S(1)}, u32[]{:S(2)}, u32[]{:S(2)}) collective-permute-start(s16[528,128]{1,0:T(8,128)(2,1)S(1)} %get-tuple-element.47), channel_id=1, source_target_pairs={{0,4},{1,29},{2,6},{3,31},{4,8},{5,1},{6,10},{7,3},{8,12},{9,5},{1... | collective-permute-start | bytes 405512 | tf_op jit(solution)/shard_map/ppermute | solution.py:45
  49.6 1.3 %collective-permute-start.11 = (s16[528,128]{1,0:T(8,128)(2,1)S(1)}, s16[528,128]{1,0:T(8,128)(2,1)S(1)}, u32[]{:S(2)}, u32[]{:S(2)}) collective-permute-start(s16[528,128]{1,0:T(8,128)(2,1)S(1)} %get-tuple-element.48), channel_id=1, source_target_pairs={{0,8},{1,25},{2,10},{3,27},{4,12},{5,29},{6,14},{7,31},{8,16},{9,1... | collective-permute-start | bytes 405512 | tf_op jit(solution)/shard_map/ppermute | solution.py:45
  50.9 0.4 collective-permute-start.12
  51.3 4.5 %collective-permute-start.13 = (s16[272,128]{1,0:T(8,128)(2,1)S(1)}, s16[272,128]{1,0:T(8,128)(2,1)S(1)}, u32[]{:S(2)}, u32[]{:S(2)}) collective-permute-start(s16[272,128]{1,0:T(8,128)(2,1)S(1)} %get-tuple-element.50), channel_id=1, source_target_pairs={{0,16},{1,17},{2,18},{3,19},{4,20},{5,21},{6,22},{7,23},{8,24},{9,... | collective-permute-start | bytes 208904 | tf_op jit(solution)/shard_map/ppermute | solution.py:45
  55.8 6.3 %collective-permute-done.13.four = s16[272,128]{1,0:T(8,128)(2,1)S(1)} collective-permute-done((s16[272,128]{1,0:T(8,128)(2,1)S(1)}, s16[272,128]{1,0:T(8,128)(2,1)S(1)}, u32[]{:S(2)}, u32[]{:S(2)}) %collective-permute-start.13) | collective-permute-done | bytes 69664 | tf_op jit(solution)/shard_map/ppermute | solution.py:45
  62.1 0.0 collective-permute-done.10.one
  62.1 0.0 collective-permute-done.11.two
  62.1 0.0 collective-permute-done.12.three
  62.1 0.7 shard_map.53
  62.8 1.3 %collective-permute-start.14 = (f32[2,16,1024]{2,1,0:T(8,128)S(1)}, f32[2,16,1024]{2,1,0:T(8,128)S(1)}, u32[]{:S(2)}, u32[]{:S(2)}) collective-permute-start(f32[2,16,1024]{2,1,0:T(8,128)S(1)} %get-tuple-element.52), channel_id=1, source_target_pairs={{0,2},{1,3},{2,0},{3,1},{4,6},{5,7},{6,4},{7,5},{8,10},{9,11},{10,... | collective-permute-start | bytes 393224 | tf_op jit(solution)/shard_map/ppermute | solution.py:45
  64.0 0.0 collective-permute-done.8.come
  64.0 0.8 shard_map.50
  64.9 0.7 collective-permute-start.15
  65.5 5.0 %collective-permute-start.16 = (s16[272,128]{1,0:T(8,128)(2,1)S(1)}, s16[272,128]{1,0:T(8,128)(2,1)S(1)}, u32[]{:S(2)}, u32[]{:S(2)}) collective-permute-start(s16[272,128]{1,0:T(8,128)(2,1)S(1)} %get-tuple-element.54), channel_id=1, source_target_pairs={{0,8},{1,25},{2,10},{3,27},{4,12},{5,29},{6,14},{7,31},{8,16},{9,1... | collective-permute-start | bytes 208904 | tf_op jit(solution)/shard_map/ppermute | solution.py:45
  70.6 0.2 collective-permute-start.17
  70.8 3.5 %collective-permute-start.18 = (s16[144,128]{1,0:T(8,128)(2,1)S(1)}, s16[144,128]{1,0:T(8,128)(2,1)S(1)}, u32[]{:S(2)}, u32[]{:S(2)}) collective-permute-start(s16[144,128]{1,0:T(8,128)(2,1)S(1)} %get-tuple-element.56), channel_id=1, source_target_pairs={{0,16},{1,17},{2,18},{3,19},{4,20},{5,21},{6,22},{7,23},{8,24},{9,... | collective-permute-start | bytes 110600 | tf_op jit(solution)/shard_map/ppermute | solution.py:45
  74.3 0.0 collective-permute-done.14.got
  74.3 3.2 %collective-permute-done.18.four = s16[144,128]{1,0:T(8,128)(2,1)S(1)} collective-permute-done((s16[144,128]{1,0:T(8,128)(2,1)S(1)}, s16[144,128]{1,0:T(8,128)(2,1)S(1)}, u32[]{:S(2)}, u32[]{:S(2)}) %collective-permute-start.18) | collective-permute-done | bytes 36896 | tf_op jit(solution)/shard_map/ppermute | solution.py:45
  77.5 0.0 collective-permute-done.15.one
  77.5 0.0 collective-permute-done.16.two
  77.5 0.0 collective-permute-done.17.three
  77.5 0.6 shard_map.54
  78.2 6.1 %collective-permute-start.19 = (f32[2,16,1024]{2,1,0:T(8,128)S(1)}, f32[2,16,1024]{2,1,0:T(8,128)S(1)}, u32[]{:S(2)}, u32[]{:S(2)}) collective-permute-start(f32[2,16,1024]{2,1,0:T(8,128)S(1)} %get-tuple-element.58), channel_id=1, source_target_pairs={{0,1},{1,0},{2,3},{3,2},{4,5},{5,4},{6,7},{7,6},{8,9},{9,8},{10,11... | collective-permute-start | bytes 393224 | tf_op jit(solution)/shard_map/ppermute | solution.py:45
  84.3 1.0 %collective-permute-done.19 = f32[2,16,1024]{2,1,0:T(8,128)S(1)} collective-permute-done((f32[2,16,1024]{2,1,0:T(8,128)S(1)}, f32[2,16,1024]{2,1,0:T(8,128)S(1)}, u32[]{:S(2)}, u32[]{:S(2)}) %collective-permute-start.19) | collective-permute-done | bytes 131104 | tf_op jit(solution)/shard_map/ppermute | solution.py:45
  85.3 0.7 add.3
Async XLA Ops:
  0.0 9.0 %collective-permute-start.5 = (bf16[64,2048]{1,0:T(8,128)(2,1)}, bf16[64,2048]{1,0:T(8,128)(2,1)S(1)}, u32[]{:S(2)}, u32[]{:S(2)}) collective-permute-start(bf16[64,2048]{1,0:T(8,128)(2,1)} %low.1), channel_id=1, source_target_pairs={{0,128},{1,129},{2,130},{3,131},{4,132},{5,133},{6,134},{7,135},{8... | collective-permute-start | bytes 786440 | tf_op jit(solution)/shard_map/ppermute | solution.py:45
  3.7 10.7 %collective-permute-start.1 = (bf16[64,2048]{1,0:T(8,128)(2,1)}, bf16[64,2048]{1,0:T(8,128)(2,1)S(1)}, u32[]{:S(2)}, u32[]{:S(2)}) collective-permute-start(bf16[64,2048]{1,0:T(8,128)(2,1)} %low.1), channel_id=1, source_target_pairs={{0,32},{1,33},{2,34},{3,35},{4,36},{5,37},{6,38},{7,39},{8,40},{9,... | collective-permute-start | bytes 786440 | tf_op jit(solution)/shard_map/ppermute | solution.py:45
  9.0 15.2 %collective-permute-start.6 = (bf16[64,2048]{1,0:T(8,128)(2,1)S(1)}, bf16[64,2048]{1,0:T(8,128)(2,1)S(1)}, u32[]{:S(2)}, u32[]{:S(2)}) collective-permute-start(bf16[64,2048]{1,0:T(8,128)(2,1)S(1)} %collective-permute-done.5.low), channel_id=1, source_target_pairs={{0,32},{1,33},{2,34},{3,35},{4,36},{5,37},{6,38},{7,39},{8,40},{9,... | collective-permute-start | bytes 786440 | tf_op jit(solution)/shard_map/ppermute | solution.py:45
  10.9 16.5 %collective-permute-start.3 = (bf16[64,2048]{1,0:T(8,128)(2,1)}, bf16[64,2048]{1,0:T(8,128)(2,1)S(1)}, u32[]{:S(2)}, u32[]{:S(2)}) collective-permute-start(bf16[64,2048]{1,0:T(8,128)(2,1)} %low.1), channel_id=1, source_target_pairs={{0,192},{1,193},{2,194},{3,195},{4,196},{5,197},{6,198},{7,199},{8... | collective-permute-start | bytes 786440 | tf_op jit(solution)/shard_map/ppermute | solution.py:45
  13.7 13.7 %collective-permute-start = (bf16[64,2048]{1,0:T(8,128)(2,1)}, bf16[64,2048]{1,0:T(8,128)(2,1)S(1)}, u32[]{:S(2)}, u32[]{:S(2)}) collective-permute-start(bf16[64,2048]{1,0:T(8,128)(2,1)} %low.1), channel_id=1, source_target_pairs={{0,64},{1,65},{2,66},{3,67},{4,68},{5,69},{6,70},{7,71},{8,72},{9,... | collective-permute-start | bytes 786440 | tf_op jit(solution)/shard_map/ppermute | solution.py:45
  14.4 13.0 %collective-permute-start.4 = (bf16[64,2048]{1,0:T(8,128)(2,1)S(1)}, bf16[64,2048]{1,0:T(8,128)(2,1)S(1)}, u32[]{:S(2)}, u32[]{:S(2)}) collective-permute-start(bf16[64,2048]{1,0:T(8,128)(2,1)S(1)} %collective-permute-done.1.high), channel_id=1, source_target_pairs={{0,192},{1,193},{2,194},{3,195},{4,196},{5,197},{6,198},{7,199},{8... | collective-permute-start | bytes 786440 | tf_op jit(solution)/shard_map/ppermute | solution.py:45
  17.2 10.2 %collective-permute-start.2 = (bf16[64,2048]{1,0:T(8,128)(2,1)S(1)}, bf16[64,2048]{1,0:T(8,128)(2,1)S(1)}, u32[]{:S(2)}, u32[]{:S(2)}) collective-permute-start(bf16[64,2048]{1,0:T(8,128)(2,1)S(1)} %collective-permute-done.1.high), channel_id=1, source_target_pairs={{0,64},{1,65},{2,66},{3,67},{4,68},{5,69},{6,70},{7,71},{8,72},{9,... | collective-permute-start | bytes 786440 | tf_op jit(solution)/shard_map/ppermute | solution.py:45
  17.2 1.0 %copy-start = (bf16[64,2048]{1,0:T(8,128)(2,1)S(1)}, bf16[64,2048]{1,0:T(8,128)(2,1)}, u32[]{:S(2)}) copy-start(bf16[64,2048]{1,0:T(8,128)(2,1)} %low.1) | copy-start | bytes 786436
  32.3 7.2 %collective-permute-start.7 = (f32[2,8,16,1024]{3,2,1,0:T(8,128)S(1)}, f32[2,8,16,1024]{3,2,1,0:T(8,128)S(1)}, u32[]{:S(2)}, u32[]{:S(2)}) collective-permute-start(f32[2,8,16,1024]{3,2,1,0:T(8,128)S(1)} %get-tuple-element.36), channel_id=1, source_target_pairs={{0,1},{1,0},{2,3},{3,2},{4,5},{5,4},{6,7},{7,6},{8,9},{9,8},{10,11... | collective-permute-start | bytes 3145736 | tf_op jit(solution)/shard_map/ppermute | solution.py:45
  39.2 3.8 %collective-permute-start.9 = (f32[2,8,16,1024]{3,2,1,0:T(8,128)S(1)}, f32[2,8,16,1024]{3,2,1,0:T(8,128)S(1)}, u32[]{:S(2)}, u32[]{:S(2)}) collective-permute-start(f32[2,8,16,1024]{3,2,1,0:T(8,128)S(1)} %get-tuple-element.45), channel_id=1, source_target_pairs={{0,1},{1,0},{2,3},{3,2},{4,5},{5,4},{6,7},{7,6},{8,9},{9,8},{10,11... | collective-permute-start | bytes 3145736 | tf_op jit(solution)/shard_map/ppermute | solution.py:45
  40.5 23.6 %collective-permute-start.8 = (s16[1040,128]{1,0:T(8,128)(2,1)S(1)}, s16[1040,128]{1,0:T(8,128)(2,1)S(1)}, u32[]{:S(2)}, u32[]{:S(2)}) collective-permute-start(s16[1040,128]{1,0:T(8,128)(2,1)S(1)} %get-tuple-element.38), channel_id=1, source_target_pairs={{0,2},{1,3},{2,0},{3,1},{4,6},{5,7},{6,4},{7,5},{8,10},{9,11},{10,... | collective-permute-start | bytes 798728 | tf_op jit(solution)/shard_map/ppermute | solution.py:45
  44.0 18.1 %collective-permute-start.10 = (s16[528,128]{1,0:T(8,128)(2,1)S(1)}, s16[528,128]{1,0:T(8,128)(2,1)S(1)}, u32[]{:S(2)}, u32[]{:S(2)}) collective-permute-start(s16[528,128]{1,0:T(8,128)(2,1)S(1)} %get-tuple-element.47), channel_id=1, source_target_pairs={{0,4},{1,29},{2,6},{3,31},{4,8},{5,1},{6,10},{7,3},{8,12},{9,5},{1... | collective-permute-start | bytes 405512 | tf_op jit(solution)/shard_map/ppermute | solution.py:45
  49.6 12.5 %collective-permute-start.11 = (s16[528,128]{1,0:T(8,128)(2,1)S(1)}, s16[528,128]{1,0:T(8,128)(2,1)S(1)}, u32[]{:S(2)}, u32[]{:S(2)}) collective-permute-start(s16[528,128]{1,0:T(8,128)(2,1)S(1)} %get-tuple-element.48), channel_id=1, source_target_pairs={{0,8},{1,25},{2,10},{3,27},{4,12},{5,29},{6,14},{7,31},{8,16},{9,1... | collective-permute-start | bytes 405512 | tf_op jit(solution)/shard_map/ppermute | solution.py:45
  50.9 11.2 %collective-permute-start.12 = (s16[528,128]{1,0:T(8,128)(2,1)S(1)}, s16[528,128]{1,0:T(8,128)(2,1)S(1)}, u32[]{:S(2)}, u32[]{:S(2)}) collective-permute-start(s16[528,128]{1,0:T(8,128)(2,1)S(1)} %get-tuple-element.49), channel_id=1, source_target_pairs={{0,12},{1,21},{2,14},{3,23},{4,16},{5,25},{6,18},{7,27},{8,20},{9,... | collective-permute-start | bytes 405512 | tf_op jit(solution)/shard_map/ppermute | solution.py:45
  51.3 10.8 %collective-permute-start.13 = (s16[272,128]{1,0:T(8,128)(2,1)S(1)}, s16[272,128]{1,0:T(8,128)(2,1)S(1)}, u32[]{:S(2)}, u32[]{:S(2)}) collective-permute-start(s16[272,128]{1,0:T(8,128)(2,1)S(1)} %get-tuple-element.50), channel_id=1, source_target_pairs={{0,16},{1,17},{2,18},{3,19},{4,20},{5,21},{6,22},{7,23},{8,24},{9,... | collective-permute-start | bytes 208904 | tf_op jit(solution)/shard_map/ppermute | solution.py:45
  62.8 11.5 %collective-permute-start.14 = (f32[2,16,1024]{2,1,0:T(8,128)S(1)}, f32[2,16,1024]{2,1,0:T(8,128)S(1)}, u32[]{:S(2)}, u32[]{:S(2)}) collective-permute-start(f32[2,16,1024]{2,1,0:T(8,128)S(1)} %get-tuple-element.52), channel_id=1, source_target_pairs={{0,2},{1,3},{2,0},{3,1},{4,6},{5,7},{6,4},{7,5},{8,10},{9,11},{10,... | collective-permute-start | bytes 393224 | tf_op jit(solution)/shard_map/ppermute | solution.py:45
  64.9 12.6 %collective-permute-start.15 = (s16[272,128]{1,0:T(8,128)(2,1)S(1)}, s16[272,128]{1,0:T(8,128)(2,1)S(1)}, u32[]{:S(2)}, u32[]{:S(2)}) collective-permute-start(s16[272,128]{1,0:T(8,128)(2,1)S(1)} %get-tuple-element.53), channel_id=1, source_target_pairs={{0,4},{1,29},{2,6},{3,31},{4,8},{5,1},{6,10},{7,3},{8,12},{9,5},{1... | collective-permute-start | bytes 208904 | tf_op jit(solution)/shard_map/ppermute | solution.py:45
  65.5 12.0 %collective-permute-start.16 = (s16[272,128]{1,0:T(8,128)(2,1)S(1)}, s16[272,128]{1,0:T(8,128)(2,1)S(1)}, u32[]{:S(2)}, u32[]{:S(2)}) collective-permute-start(s16[272,128]{1,0:T(8,128)(2,1)S(1)} %get-tuple-element.54), channel_id=1, source_target_pairs={{0,8},{1,25},{2,10},{3,27},{4,12},{5,29},{6,14},{7,31},{8,16},{9,1... | collective-permute-start | bytes 208904 | tf_op jit(solution)/shard_map/ppermute | solution.py:45
  70.6 6.9 %collective-permute-start.17 = (s16[272,128]{1,0:T(8,128)(2,1)S(1)}, s16[272,128]{1,0:T(8,128)(2,1)S(1)}, u32[]{:S(2)}, u32[]{:S(2)}) collective-permute-start(s16[272,128]{1,0:T(8,128)(2,1)S(1)} %get-tuple-element.55), channel_id=1, source_target_pairs={{0,12},{1,21},{2,14},{3,23},{4,16},{5,25},{6,18},{7,27},{8,20},{9,... | collective-permute-start | bytes 208904 | tf_op jit(solution)/shard_map/ppermute | solution.py:45
  70.8 6.7 %collective-permute-start.18 = (s16[144,128]{1,0:T(8,128)(2,1)S(1)}, s16[144,128]{1,0:T(8,128)(2,1)S(1)}, u32[]{:S(2)}, u32[]{:S(2)}) collective-permute-start(s16[144,128]{1,0:T(8,128)(2,1)S(1)} %get-tuple-element.56), channel_id=1, source_target_pairs={{0,16},{1,17},{2,18},{3,19},{4,20},{5,21},{6,22},{7,23},{8,24},{9,... | collective-permute-start | bytes 110600 | tf_op jit(solution)/shard_map/ppermute | solution.py:45
  78.2 7.1 %collective-permute-start.19 = (f32[2,16,1024]{2,1,0:T(8,128)S(1)}, f32[2,16,1024]{2,1,0:T(8,128)S(1)}, u32[]{:S(2)}, u32[]{:S(2)}) collective-permute-start(f32[2,16,1024]{2,1,0:T(8,128)S(1)} %get-tuple-element.58), channel_id=1, source_target_pairs={{0,1},{1,0},{2,3},{3,2},{4,5},{5,4},{6,7},{7,6},{8,9},{9,8},{10,11... | collective-permute-start | bytes 393224 | tf_op jit(solution)/shard_map/ppermute | solution.py:45

commit v3 on v2

--- a/solution.py
+++ b/solution.py
@@ -100,16 +100,13 @@
         after[...] = product(info, tile, (0,), staged, (shifted,))
 
 
-def middle_body(turn, info, low, high, staged, before, after, shifted):
-    build_shifted(info, low, high, shifted)
-    after[...] = before[...] + product(info, 0, (turn,), staged, (shifted,))
-
-
-def last_body(turns, info, low0, high0, low1, high1, staged, before, keep, send, shifted0, shifted1, sums):
-    build_shifted(info, low0, high0, shifted0)
-    build_shifted(info, low1, high1, shifted1)
-    total = before[...] + product(info, 0, turns, staged, (shifted0, shifted1))
-    split(info, 0, total, keep, send, sums)
+def last_body(turns, info, *refs):
+    count = len(turns)
+    sources, (staged, before, keep, send) = refs[: 2 * count], refs[2 * count : 2 * count + 4]
+    copies, sums = refs[2 * count + 4 : -1], refs[-1]
+    for index, shifted in enumerate(copies):
+        build_shifted(info, sources[2 * index], sources[2 * index + 1], shifted)
+    split(info, 0, before[...] + product(info, 0, turns, staged, copies), keep, send, sums)
 
 
 def rest_body(turns, info, staged, before, *refs):
@@ -265,13 +262,11 @@
         FIRST_LIMIT,
         2,
     )
-    run = functools.partial(middle_body, 2)
-    operands = [info, two, two_far, staged, sum0]
-    sum0, two_copies = call(run, [TOTAL, COPIES], operands, blocks=1, aliases={4: 0})
     sums = [pltpu.VMEM((B, COLS), jnp.float32)]
-    run = functools.partial(last_body, (3, 1))
-    operands = [info, up, up_far, down, down_far, staged, sum0]
-    keep0, send0, up_copies, down_copies = call(run, [PARTS, PARTS, COPIES, COPIES], operands, sums, blocks=2)
+    run = functools.partial(last_body, (2, 3, 1))
+    operands = [info, two, two_far, up, up_far, down, down_far, staged, sum0]
+    outs = [PARTS, PARTS, COPIES, COPIES, COPIES]
+    keep0, send0, two_copies, up_copies, down_copies = call(run, outs, operands, sums, blocks=3)
     get0 = shift(send0, dc=1)
     run = functools.partial(rest_body, (2, 3, 1))
     operands = [info, staged, sum1, two_copies, up_copies, down_copies]

time: 86 us -> 81.5 us (0.948)
  starting transfers between devices: 46.5 us -> 44.3 us
  Pallas kernels: 22.3 us -> 20.9 us
  waiting for transfers between devices: 14.6 us -> 13.7 us
    ppermute x20, starting transfers between devices: 46.5 us -> 44.3 us  [shift(): return lax.ppermute(x, AXES, route(move))]
    pallas_call x9 -> x8, Pallas kernels: 22.3 us -> 20.9 us  [call(): pl.pallas_call(run, in_specs=specs or [SMALL] + [NEAR] * (len(operands) -...]
    ppermute x20, waiting for transfers between devices: 14.6 us -> 13.7 us  [shift(): return lax.ppermute(x, AXES, route(move))]
  transfers between devices with their start and end apart: 20 -> 20, of which waited for: 4 -> 5; matrix products, arithmetic and copies ran while one was open for 1% -> 1% of each run, Pallas kernels for 20% -> 17%
where the time goes in v3:
time: 81.5 us; the launch traced here: 81.4 us
  starting transfers between devices  44.3 us (54%)
  Pallas kernels  20.9 us (26%)
  waiting for transfers between devices  13.7 us (17%)
  local copies, waits for them, and re-layouts  1.7 us (2%)
    ppermute x20, starting transfers between devices, shift(): return lax.ppermute(x, AXES, route(move))  44.3 us
    pallas_call x8, Pallas kernels, call(): pl.pallas_call(run, in_specs=specs or [SMALL] + [NEAR] * (len(operands) -...  20.9 us
    ppermute x20, waiting for transfers between devices, shift(): return lax.ppermute(x, AXES, route(move))  13.7 us
  transfers between devices with their start and end apart: 20, of which 5 were waited for; matrix products, arithmetic and copies ran while one was open for 1% of the time, Pallas kernels for 17%

profile of v3, /device:TPU:1, one launch (start us, length us, event | category | flops | bytes accessed | tf_op | source)
XLA Modules:
  0.0 81.4 jit_solution(6611888516682636660)
XLA Ops:
  0.0 2.0 %collective-permute-start.3 = (bf16[64,2048]{1,0:T(8,128)(2,1)}, bf16[64,2048]{1,0:T(8,128)(2,1)S(1)}, u32[]{:S(2)}, u32[]{:S(2)}) collective-permute-start(bf16[64,2048]{1,0:T(8,128)(2,1)} %low.1), channel_id=1, source_target_pairs={{0,32},{1,33},{2,34},{3,35},{4,36},{5,37},{6,38},{7,39},{8,40},{9,... | collective-permute-start | bytes 786440 | tf_op jit(solution)/shard_map/ppermute | solution.py:45
  2.0 2.9 %collective-permute-start = (bf16[64,2048]{1,0:T(8,128)(2,1)}, bf16[64,2048]{1,0:T(8,128)(2,1)S(1)}, u32[]{:S(2)}, u32[]{:S(2)}) collective-permute-start(bf16[64,2048]{1,0:T(8,128)(2,1)} %low.1), channel_id=1, source_target_pairs={{0,128},{1,129},{2,130},{3,131},{4,132},{5,133},{6,134},{7,135},{8... | collective-permute-start | bytes 786440 | tf_op jit(solution)/shard_map/ppermute | solution.py:45
  4.9 0.4 collective-permute-start.2
  5.3 2.3 %collective-permute-start.5 = (bf16[64,2048]{1,0:T(8,128)(2,1)}, bf16[64,2048]{1,0:T(8,128)(2,1)S(1)}, u32[]{:S(2)}, u32[]{:S(2)}) collective-permute-start(bf16[64,2048]{1,0:T(8,128)(2,1)} %low.1), channel_id=1, source_target_pairs={{0,192},{1,193},{2,194},{3,195},{4,196},{5,197},{6,198},{7,199},{8... | collective-permute-start | bytes 786440 | tf_op jit(solution)/shard_map/ppermute | solution.py:45
  7.6 0.0 collective-permute-done.3.high
  7.6 3.3 %collective-permute-start.6 = (bf16[64,2048]{1,0:T(8,128)(2,1)S(1)}, bf16[64,2048]{1,0:T(8,128)(2,1)S(1)}, u32[]{:S(2)}, u32[]{:S(2)}) collective-permute-start(bf16[64,2048]{1,0:T(8,128)(2,1)S(1)} %collective-permute-done.3.high), channel_id=1, source_target_pairs={{0,192},{1,193},{2,194},{3,195},{4,196},{5,197},{6,198},{7,199},{8... | collective-permute-start | bytes 786440 | tf_op jit(solution)/shard_map/ppermute | solution.py:45
  11.0 0.0 collective-permute-start.4
  11.0 0.0 collective-permute-done.refs_0_
  11.0 1.2 %collective-permute-start.1 = (bf16[64,2048]{1,0:T(8,128)(2,1)S(1)}, bf16[64,2048]{1,0:T(8,128)(2,1)S(1)}, u32[]{:S(2)}, u32[]{:S(2)}) collective-permute-start(bf16[64,2048]{1,0:T(8,128)(2,1)S(1)} %collective-permute-done.refs_0_), channel_id=1, source_target_pairs={{0,32},{1,33},{2,34},{3,35},{4,36},{5,37},{6,38},{7,39},{8,40},{9,... | collective-permute-start | bytes 786440 | tf_op jit(solution)/shard_map/ppermute | solution.py:45
  12.2 0.7 concatenate.3.info
  12.9 0.0 copy-start
  12.9 1.0 %copy-done = bf16[64,2048]{1,0:T(8,128)(2,1)S(1)} copy-done((bf16[64,2048]{1,0:T(8,128)(2,1)S(1)}, bf16[64,2048]{1,0:T(8,128)(2,1)}, u32[]{:S(2)}) %copy-start) | copy-done | bytes 262168
  13.9 6.1 %shard_map.46 = (f32[512,1024]{1,0:T(8,128)S(1)}, f32[512,1024]{1,0:T(8,128)S(1)}, bf16[2,512,4096]{2,1,0:T(8,128)(2,1)S(1)}) custom-call(s32[10]{0:T(128)S(1)} %concatenate.3.info, bf16[64,2048]{1,0:T(8,128)(2,1)S(1)} %copy-done, bf16[64,2048]{1,0:T(8,128)(2,1)S(1)} %collective-permute-done.3.high, bf16[2,1,512,4096]{3,2,1,0:T(8,128)(2,1)} %kernel.1), custom_call_target="tpu_custom_call" | custom-call | flops 2147483648 | bytes 4194304 | tf_op jit(solution)/shard_map/pallas_call | solution.py:125
  20.0 0.0 collective-permute-done.2.refs_2_
  20.0 0.0 collective-permute-done.5.refs_4_
  20.0 2.4 %collective-permute-done.6.refs_5_ = bf16[64,2048]{1,0:T(8,128)(2,1)S(1)} collective-permute-done((bf16[64,2048]{1,0:T(8,128)(2,1)S(1)}, bf16[64,2048]{1,0:T(8,128)(2,1)S(1)}, u32[]{:S(2)}, u32[]{:S(2)}) %collective-permute-start.6) | collective-permute-done | bytes 262176 | tf_op jit(solution)/shard_map/ppermute | solution.py:45
  22.5 0.7 collective-permute-done.4.refs_3_
  23.2 0.0 collective-permute-done.1.refs_1_
  23.2 6.6 %shard_map.47 = (f32[2,8,16,1024]{3,2,1,0:T(8,128)S(1)}, f32[2,8,16,1024]{3,2,1,0:T(8,128)S(1)}, bf16[8,128,3072]{2,1,0:T(8,128)(2,1)S(1)}, bf16[8,128,3072]{2,1,0:T(8,128)(2,1)S(1)}, bf16[8,128,3072]{2,1,0:T(8,128)(2,1)S(1)}) custom-call(s32[10]{0:T(128)S(1)} %concatenate.3.info, bf16[64,2048]{1,0:T(8,128)(2,1)S(1)} %collective-permute-done.refs_0_, ...), custom_call_target="tpu_custom_call" | custom-call | flops 3221225472 | bytes 4194304 | tf_op jit(solution)/shard_map/pallas_call | solution.py:125
  29.8 1.0 %collective-permute-start.7 = (f32[2,8,16,1024]{3,2,1,0:T(8,128)S(1)}, f32[2,8,16,1024]{3,2,1,0:T(8,128)S(1)}, u32[]{:S(2)}, u32[]{:S(2)}) collective-permute-start(f32[2,8,16,1024]{3,2,1,0:T(8,128)S(1)} %get-tuple-element.34), channel_id=1, source_target_pairs={{0,1},{1,0},{2,3},{3,2},{4,5},{5,4},{6,7},{7,6},{8,9},{9,8},{10,11... | collective-permute-start | bytes 3145736 | tf_op jit(solution)/shard_map/ppermute | solution.py:45
  30.8 4.2 %shard_map.50 = (f32[2,8,16,1024]{3,2,1,0:T(8,128)S(1)}, f32[2,8,16,1024]{3,2,1,0:T(8,128)S(1)}) custom-call(s32[10]{0:T(128)S(1)} %concatenate.3.info, bf16[2,512,4096]{2,1,0:T(8,128)(2,1)S(1)} %get-tuple-element.31.refs_6_.staged, f32[512,1024]{1,0:T(8,128)S(1)} %get-tuple-element.38.before, bf16[8,128,3072]{2,1,0:T(8,128)(2,1)S(1)} %get-tuple-element.39.refs_0_, ...), custom_call_target="tpu_custom_call" | custom-call | flops 3221225472 | bytes 4194304 | tf_op jit(solution)/shard_map/pallas_call | solution.py:125
  34.9 0.1 collective-permute-start.9
  35.0 0.0 collective-permute-done.7.get
  35.0 0.9 %shard_map.48 = (f32[8,16,1024]{2,1,0:T(8,128)S(1)}, s16[1040,128]{1,0:T(8,128)(2,1)S(1)}) custom-call(s32[10]{0:T(128)S(1)} %concatenate.3.info, f32[2,8,16,1024]{3,2,1,0:T(8,128)S(1)} %get-tuple-element.33.keep, f32[2,8,16,1024]{3,2,1,0:T(8,128)S(1)} %collective-permute-done.7.get), custom_call_target="tpu_custom_call" | custom-call | bytes 1048576 | tf_op jit(solution)/shard_map/pallas_call | solution.py:125
  35.9 2.8 %collective-permute-start.8 = (s16[1040,128]{1,0:T(8,128)(2,1)S(1)}, s16[1040,128]{1,0:T(8,128)(2,1)S(1)}, u32[]{:S(2)}, u32[]{:S(2)}) collective-permute-start(s16[1040,128]{1,0:T(8,128)(2,1)S(1)} %get-tuple-element.36), channel_id=1, source_target_pairs={{0,2},{1,3},{2,0},{3,1},{4,6},{5,7},{6,4},{7,5},{8,10},{9,11},{10,... | collective-permute-start | bytes 798728 | tf_op jit(solution)/shard_map/ppermute | solution.py:45
  38.7 0.0 collective-permute-done.9.get
  38.7 1.0 %shard_map.51 = (s16[528,128]{1,0:T(8,128)(2,1)S(1)}, s16[528,128]{1,0:T(8,128)(2,1)S(1)}, s16[528,128]{1,0:T(8,128)(2,1)S(1)}, s16[272,128]{1,0:T(8,128)(2,1)S(1)}, f32[2,16,1024]{2,1,0:T(8,128)S(1)}) custom-call(s32[10]{0:T(128)S(1)} %concatenate.3.info, f32[2,8,16,1024]{3,2,1,0:T(8,128)S(1)} %get-tuple-element.42.keep, ...), custom_call_target="tpu_custom_call" | custom-call | bytes 1048576 | tf_op jit(solution)/shard_map/pallas_call | solution.py:125
  39.7 5.6 %collective-permute-start.10 = (s16[528,128]{1,0:T(8,128)(2,1)S(1)}, s16[528,128]{1,0:T(8,128)(2,1)S(1)}, u32[]{:S(2)}, u32[]{:S(2)}) collective-permute-start(s16[528,128]{1,0:T(8,128)(2,1)S(1)} %get-tuple-element.45), channel_id=1, source_target_pairs={{0,4},{1,29},{2,6},{3,31},{4,8},{5,1},{6,10},{7,3},{8,12},{9,5},{1... | collective-permute-start | bytes 405512 | tf_op jit(solution)/shard_map/ppermute | solution.py:45
  45.3 1.2 %collective-permute-start.11 = (s16[528,128]{1,0:T(8,128)(2,1)S(1)}, s16[528,128]{1,0:T(8,128)(2,1)S(1)}, u32[]{:S(2)}, u32[]{:S(2)}) collective-permute-start(s16[528,128]{1,0:T(8,128)(2,1)S(1)} %get-tuple-element.46), channel_id=1, source_target_pairs={{0,8},{1,25},{2,10},{3,27},{4,12},{5,29},{6,14},{7,31},{8,16},{9,1... | collective-permute-start | bytes 405512 | tf_op jit(solution)/shard_map/ppermute | solution.py:45
  46.6 0.4 collective-permute-start.12
  47.0 4.5 %collective-permute-start.13 = (s16[272,128]{1,0:T(8,128)(2,1)S(1)}, s16[272,128]{1,0:T(8,128)(2,1)S(1)}, u32[]{:S(2)}, u32[]{:S(2)}) collective-permute-start(s16[272,128]{1,0:T(8,128)(2,1)S(1)} %get-tuple-element.48), channel_id=1, source_target_pairs={{0,16},{1,17},{2,18},{3,19},{4,20},{5,21},{6,22},{7,23},{8,24},{9,... | collective-permute-start | bytes 208904 | tf_op jit(solution)/shard_map/ppermute | solution.py:45
  51.5 6.3 %collective-permute-done.13.four = s16[272,128]{1,0:T(8,128)(2,1)S(1)} collective-permute-done((s16[272,128]{1,0:T(8,128)(2,1)S(1)}, s16[272,128]{1,0:T(8,128)(2,1)S(1)}, u32[]{:S(2)}, u32[]{:S(2)}) %collective-permute-start.13) | collective-permute-done | bytes 69664 | tf_op jit(solution)/shard_map/ppermute | solution.py:45
  57.8 0.0 collective-permute-done.10.one
  57.8 0.0 collective-permute-done.11.two
  57.8 0.0 collective-permute-done.12.three
  57.8 0.7 shard_map.52
  58.5 1.1 %collective-permute-start.14 = (f32[2,16,1024]{2,1,0:T(8,128)S(1)}, f32[2,16,1024]{2,1,0:T(8,128)S(1)}, u32[]{:S(2)}, u32[]{:S(2)}) collective-permute-start(f32[2,16,1024]{2,1,0:T(8,128)S(1)} %get-tuple-element.50), channel_id=1, source_target_pairs={{0,2},{1,3},{2,0},{3,1},{4,6},{5,7},{6,4},{7,5},{8,10},{9,11},{10,... | collective-permute-start | bytes 393224 | tf_op jit(solution)/shard_map/ppermute | solution.py:45
  59.5 0.0 collective-permute-done.8.come
  59.5 0.8 %shard_map.49 = (s16[272,128]{1,0:T(8,128)(2,1)S(1)}, s16[272,128]{1,0:T(8,128)(2,1)S(1)}, s16[272,128]{1,0:T(8,128)(2,1)S(1)}, s16[144,128]{1,0:T(8,128)(2,1)S(1)}, f32[16,1024]{1,0:T(8,128)S(1)}) custom-call(s32[10]{0:T(128)S(1)} %concatenate.3.info, f32[8,16,1024]{2,1,0:T(8,128)S(1)} %get-tuple-element.35.own, ...), custom_call_target="tpu_custom_call" | custom-call | bytes 1048576 | tf_op jit(solution)/shard_map/pallas_call | solution.py:125
  60.4 0.6 collective-permute-start.15
  61.0 5.0 %collective-permute-start.16 = (s16[272,128]{1,0:T(8,128)(2,1)S(1)}, s16[272,128]{1,0:T(8,128)(2,1)S(1)}, u32[]{:S(2)}, u32[]{:S(2)}) collective-permute-start(s16[272,128]{1,0:T(8,128)(2,1)S(1)} %get-tuple-element.52), channel_id=1, source_target_pairs={{0,8},{1,25},{2,10},{3,27},{4,12},{5,29},{6,14},{7,31},{8,16},{9,1... | collective-permute-start | bytes 208904 | tf_op jit(solution)/shard_map/ppermute | solution.py:45
  66.0 0.2 collective-permute-start.17
  66.2 3.6 %collective-permute-start.18 = (s16[144,128]{1,0:T(8,128)(2,1)S(1)}, s16[144,128]{1,0:T(8,128)(2,1)S(1)}, u32[]{:S(2)}, u32[]{:S(2)}) collective-permute-start(s16[144,128]{1,0:T(8,128)(2,1)S(1)} %get-tuple-element.54), channel_id=1, source_target_pairs={{0,16},{1,17},{2,18},{3,19},{4,20},{5,21},{6,22},{7,23},{8,24},{9,... | collective-permute-start | bytes 110600 | tf_op jit(solution)/shard_map/ppermute | solution.py:45
  69.7 0.0 collective-permute-done.14.got
  69.8 3.2 %collective-permute-done.18.four = s16[144,128]{1,0:T(8,128)(2,1)S(1)} collective-permute-done((s16[144,128]{1,0:T(8,128)(2,1)S(1)}, s16[144,128]{1,0:T(8,128)(2,1)S(1)}, u32[]{:S(2)}, u32[]{:S(2)}) %collective-permute-start.18) | collective-permute-done | bytes 36896 | tf_op jit(solution)/shard_map/ppermute | solution.py:45
  72.9 0.0 collective-permute-done.15.one
  72.9 0.0 collective-permute-done.16.two
  72.9 0.0 collective-permute-done.17.three
  73.0 0.6 shard_map.53
  73.6 6.1 %collective-permute-start.19 = (f32[2,16,1024]{2,1,0:T(8,128)S(1)}, f32[2,16,1024]{2,1,0:T(8,128)S(1)}, u32[]{:S(2)}, u32[]{:S(2)}) collective-permute-start(f32[2,16,1024]{2,1,0:T(8,128)S(1)} %get-tuple-element.56), channel_id=1, source_target_pairs={{0,1},{1,0},{2,3},{3,2},{4,5},{5,4},{6,7},{7,6},{8,9},{9,8},{10,11... | collective-permute-start | bytes 393224 | tf_op jit(solution)/shard_map/ppermute | solution.py:45
  79.7 1.0 %collective-permute-done.19 = f32[2,16,1024]{2,1,0:T(8,128)S(1)} collective-permute-done((f32[2,16,1024]{2,1,0:T(8,128)S(1)}, f32[2,16,1024]{2,1,0:T(8,128)S(1)}, u32[]{:S(2)}, u32[]{:S(2)}) %collective-permute-start.19) | collective-permute-done | bytes 131104 | tf_op jit(solution)/shard_map/ppermute | solution.py:45
  80.7 0.7 add.3
Async XLA Ops:
  0.0 7.6 %collective-permute-start.3 = (bf16[64,2048]{1,0:T(8,128)(2,1)}, bf16[64,2048]{1,0:T(8,128)(2,1)S(1)}, u32[]{:S(2)}, u32[]{:S(2)}) collective-permute-start(bf16[64,2048]{1,0:T(8,128)(2,1)} %low.1), channel_id=1, source_target_pairs={{0,32},{1,33},{2,34},{3,35},{4,36},{5,37},{6,38},{7,39},{8,40},{9,... | collective-permute-start | bytes 786440 | tf_op jit(solution)/shard_map/ppermute | solution.py:45
  2.0 8.9 %collective-permute-start = (bf16[64,2048]{1,0:T(8,128)(2,1)}, bf16[64,2048]{1,0:T(8,128)(2,1)S(1)}, u32[]{:S(2)}, u32[]{:S(2)}) collective-permute-start(bf16[64,2048]{1,0:T(8,128)(2,1)} %low.1), channel_id=1, source_target_pairs={{0,128},{1,129},{2,130},{3,131},{4,132},{5,133},{6,134},{7,135},{8... | collective-permute-start | bytes 786440 | tf_op jit(solution)/shard_map/ppermute | solution.py:45
  4.9 15.1 %collective-permute-start.2 = (bf16[64,2048]{1,0:T(8,128)(2,1)}, bf16[64,2048]{1,0:T(8,128)(2,1)S(1)}, u32[]{:S(2)}, u32[]{:S(2)}) collective-permute-start(bf16[64,2048]{1,0:T(8,128)(2,1)} %low.1), channel_id=1, source_target_pairs={{0,64},{1,65},{2,66},{3,67},{4,68},{5,69},{6,70},{7,71},{8,72},{9,... | collective-permute-start | bytes 786440 | tf_op jit(solution)/shard_map/ppermute | solution.py:45
  5.3 14.7 %collective-permute-start.5 = (bf16[64,2048]{1,0:T(8,128)(2,1)}, bf16[64,2048]{1,0:T(8,128)(2,1)S(1)}, u32[]{:S(2)}, u32[]{:S(2)}) collective-permute-start(bf16[64,2048]{1,0:T(8,128)(2,1)} %low.1), channel_id=1, source_target_pairs={{0,192},{1,193},{2,194},{3,195},{4,196},{5,197},{6,198},{7,199},{8... | collective-permute-start | bytes 786440 | tf_op jit(solution)/shard_map/ppermute | solution.py:45
  7.6 14.8 %collective-permute-start.6 = (bf16[64,2048]{1,0:T(8,128)(2,1)S(1)}, bf16[64,2048]{1,0:T(8,128)(2,1)S(1)}, u32[]{:S(2)}, u32[]{:S(2)}) collective-permute-start(bf16[64,2048]{1,0:T(8,128)(2,1)S(1)} %collective-permute-done.3.high), channel_id=1, source_target_pairs={{0,192},{1,193},{2,194},{3,195},{4,196},{5,197},{6,198},{7,199},{8... | collective-permute-start | bytes 786440 | tf_op jit(solution)/shard_map/ppermute | solution.py:45
  11.0 12.2 %collective-permute-start.4 = (bf16[64,2048]{1,0:T(8,128)(2,1)S(1)}, bf16[64,2048]{1,0:T(8,128)(2,1)S(1)}, u32[]{:S(2)}, u32[]{:S(2)}) collective-permute-start(bf16[64,2048]{1,0:T(8,128)(2,1)S(1)} %collective-permute-done.3.high), channel_id=1, source_target_pairs={{0,64},{1,65},{2,66},{3,67},{4,68},{5,69},{6,70},{7,71},{8,72},{9,... | collective-permute-start | bytes 786440 | tf_op jit(solution)/shard_map/ppermute | solution.py:45
  11.0 12.2 %collective-permute-start.1 = (bf16[64,2048]{1,0:T(8,128)(2,1)S(1)}, bf16[64,2048]{1,0:T(8,128)(2,1)S(1)}, u32[]{:S(2)}, u32[]{:S(2)}) collective-permute-start(bf16[64,2048]{1,0:T(8,128)(2,1)S(1)} %collective-permute-done.refs_0_), channel_id=1, source_target_pairs={{0,32},{1,33},{2,34},{3,35},{4,36},{5,37},{6,38},{7,39},{8,40},{9,... | collective-permute-start | bytes 786440 | tf_op jit(solution)/shard_map/ppermute | solution.py:45
  12.9 1.0 %copy-start = (bf16[64,2048]{1,0:T(8,128)(2,1)S(1)}, bf16[64,2048]{1,0:T(8,128)(2,1)}, u32[]{:S(2)}) copy-start(bf16[64,2048]{1,0:T(8,128)(2,1)} %low.1) | copy-start | bytes 786436
  29.8 5.3 %collective-permute-start.7 = (f32[2,8,16,1024]{3,2,1,0:T(8,128)S(1)}, f32[2,8,16,1024]{3,2,1,0:T(8,128)S(1)}, u32[]{:S(2)}, u32[]{:S(2)}) collective-permute-start(f32[2,8,16,1024]{3,2,1,0:T(8,128)S(1)} %get-tuple-element.34), channel_id=1, source_target_pairs={{0,1},{1,0},{2,3},{3,2},{4,5},{5,4},{6,7},{7,6},{8,9},{9,8},{10,11... | collective-permute-start | bytes 3145736 | tf_op jit(solution)/shard_map/ppermute | solution.py:45
  34.9 3.8 %collective-permute-start.9 = (f32[2,8,16,1024]{3,2,1,0:T(8,128)S(1)}, f32[2,8,16,1024]{3,2,1,0:T(8,128)S(1)}, u32[]{:S(2)}, u32[]{:S(2)}) collective-permute-start(f32[2,8,16,1024]{3,2,1,0:T(8,128)S(1)} %get-tuple-element.43), channel_id=1, source_target_pairs={{0,1},{1,0},{2,3},{3,2},{4,5},{5,4},{6,7},{7,6},{8,9},{9,8},{10,11... | collective-permute-start | bytes 3145736 | tf_op jit(solution)/shard_map/ppermute | solution.py:45
  35.9 23.6 %collective-permute-start.8 = (s16[1040,128]{1,0:T(8,128)(2,1)S(1)}, s16[1040,128]{1,0:T(8,128)(2,1)S(1)}, u32[]{:S(2)}, u32[]{:S(2)}) collective-permute-start(s16[1040,128]{1,0:T(8,128)(2,1)S(1)} %get-tuple-element.36), channel_id=1, source_target_pairs={{0,2},{1,3},{2,0},{3,1},{4,6},{5,7},{6,4},{7,5},{8,10},{9,11},{10,... | collective-permute-start | bytes 798728 | tf_op jit(solution)/shard_map/ppermute | solution.py:45
  39.7 18.1 %collective-permute-start.10 = (s16[528,128]{1,0:T(8,128)(2,1)S(1)}, s16[528,128]{1,0:T(8,128)(2,1)S(1)}, u32[]{:S(2)}, u32[]{:S(2)}) collective-permute-start(s16[528,128]{1,0:T(8,128)(2,1)S(1)} %get-tuple-element.45), channel_id=1, source_target_pairs={{0,4},{1,29},{2,6},{3,31},{4,8},{5,1},{6,10},{7,3},{8,12},{9,5},{1... | collective-permute-start | bytes 405512 | tf_op jit(solution)/shard_map/ppermute | solution.py:45
  45.3 12.4 %collective-permute-start.11 = (s16[528,128]{1,0:T(8,128)(2,1)S(1)}, s16[528,128]{1,0:T(8,128)(2,1)S(1)}, u32[]{:S(2)}, u32[]{:S(2)}) collective-permute-start(s16[528,128]{1,0:T(8,128)(2,1)S(1)} %get-tuple-element.46), channel_id=1, source_target_pairs={{0,8},{1,25},{2,10},{3,27},{4,12},{5,29},{6,14},{7,31},{8,16},{9,1... | collective-permute-start | bytes 405512 | tf_op jit(solution)/shard_map/ppermute | solution.py:45
  46.6 11.2 %collective-permute-start.12 = (s16[528,128]{1,0:T(8,128)(2,1)S(1)}, s16[528,128]{1,0:T(8,128)(2,1)S(1)}, u32[]{:S(2)}, u32[]{:S(2)}) collective-permute-start(s16[528,128]{1,0:T(8,128)(2,1)S(1)} %get-tuple-element.47), channel_id=1, source_target_pairs={{0,12},{1,21},{2,14},{3,23},{4,16},{5,25},{6,18},{7,27},{8,20},{9,... | collective-permute-start | bytes 405512 | tf_op jit(solution)/shard_map/ppermute | solution.py:45
  47.0 10.8 %collective-permute-start.13 = (s16[272,128]{1,0:T(8,128)(2,1)S(1)}, s16[272,128]{1,0:T(8,128)(2,1)S(1)}, u32[]{:S(2)}, u32[]{:S(2)}) collective-permute-start(s16[272,128]{1,0:T(8,128)(2,1)S(1)} %get-tuple-element.48), channel_id=1, source_target_pairs={{0,16},{1,17},{2,18},{3,19},{4,20},{5,21},{6,22},{7,23},{8,24},{9,... | collective-permute-start | bytes 208904 | tf_op jit(solution)/shard_map/ppermute | solution.py:45
  58.5 11.3 %collective-permute-start.14 = (f32[2,16,1024]{2,1,0:T(8,128)S(1)}, f32[2,16,1024]{2,1,0:T(8,128)S(1)}, u32[]{:S(2)}, u32[]{:S(2)}) collective-permute-start(f32[2,16,1024]{2,1,0:T(8,128)S(1)} %get-tuple-element.50), channel_id=1, source_target_pairs={{0,2},{1,3},{2,0},{3,1},{4,6},{5,7},{6,4},{7,5},{8,10},{9,11},{10,... | collective-permute-start | bytes 393224 | tf_op jit(solution)/shard_map/ppermute | solution.py:45
  60.4 12.6 %collective-permute-start.15 = (s16[272,128]{1,0:T(8,128)(2,1)S(1)}, s16[272,128]{1,0:T(8,128)(2,1)S(1)}, u32[]{:S(2)}, u32[]{:S(2)}) collective-permute-start(s16[272,128]{1,0:T(8,128)(2,1)S(1)} %get-tuple-element.51), channel_id=1, source_target_pairs={{0,4},{1,29},{2,6},{3,31},{4,8},{5,1},{6,10},{7,3},{8,12},{9,5},{1... | collective-permute-start | bytes 208904 | tf_op jit(solution)/shard_map/ppermute | solution.py:45
  61.0 11.9 %collective-permute-start.16 = (s16[272,128]{1,0:T(8,128)(2,1)S(1)}, s16[272,128]{1,0:T(8,128)(2,1)S(1)}, u32[]{:S(2)}, u32[]{:S(2)}) collective-permute-start(s16[272,128]{1,0:T(8,128)(2,1)S(1)} %get-tuple-element.52), channel_id=1, source_target_pairs={{0,8},{1,25},{2,10},{3,27},{4,12},{5,29},{6,14},{7,31},{8,16},{9,1... | collective-permute-start | bytes 208904 | tf_op jit(solution)/shard_map/ppermute | solution.py:45
  66.0 6.9 %collective-permute-start.17 = (s16[272,128]{1,0:T(8,128)(2,1)S(1)}, s16[272,128]{1,0:T(8,128)(2,1)S(1)}, u32[]{:S(2)}, u32[]{:S(2)}) collective-permute-start(s16[272,128]{1,0:T(8,128)(2,1)S(1)} %get-tuple-element.53), channel_id=1, source_target_pairs={{0,12},{1,21},{2,14},{3,23},{4,16},{5,25},{6,18},{7,27},{8,20},{9,... | collective-permute-start | bytes 208904 | tf_op jit(solution)/shard_map/ppermute | solution.py:45
  66.2 6.7 %collective-permute-start.18 = (s16[144,128]{1,0:T(8,128)(2,1)S(1)}, s16[144,128]{1,0:T(8,128)(2,1)S(1)}, u32[]{:S(2)}, u32[]{:S(2)}) collective-permute-start(s16[144,128]{1,0:T(8,128)(2,1)S(1)} %get-tuple-element.54), channel_id=1, source_target_pairs={{0,16},{1,17},{2,18},{3,19},{4,20},{5,21},{6,22},{7,23},{8,24},{9,... | collective-permute-start | bytes 110600 | tf_op jit(solution)/shard_map/ppermute | solution.py:45
  73.6 7.1 %collective-permute-start.19 = (f32[2,16,1024]{2,1,0:T(8,128)S(1)}, f32[2,16,1024]{2,1,0:T(8,128)S(1)}, u32[]{:S(2)}, u32[]{:S(2)}) collective-permute-start(f32[2,16,1024]{2,1,0:T(8,128)S(1)} %get-tuple-element.56), channel_id=1, source_target_pairs={{0,1},{1,0},{2,3},{3,2},{4,5},{5,4},{6,7},{7,6},{8,9},{9,8},{10,11... | collective-permute-start | bytes 393224 | tf_op jit(solution)/shard_map/ppermute | solution.py:45
